TPU v7x, 512 devices: a whole 4x4x16 slice. The times are simulated.
512 devices in a mesh: dp: 16 (over y, x_lo, core), vocab: 32 (over x_hi, z).
Axes of the slice: x: 4 (x_hi: 2, x_lo: 2; x = x_hi * 2 + x_lo), y: 4, z: 16, core: 2. Of those that a mesh axis runs over, the one named last changes fastest.
Arguments:
- hidden_states: bfloat16 [4, 4096, 8192], P(None, 'dp', 'vocab'), may hold values from -400 to 400
- exit_layers: int32 [64, 2], P('dp'), may hold values from 0 to 3, all different within a row
- targets: int32 [4096], P('dp'), may hold values from 0 to 8191
- norm_gain: bfloat16 [8192], replicated, may hold values from 0.25 to 1.75
- exit_scale: float32 [2], replicated, may hold values from 0.5 to 2
- unembedding: bfloat16 [8192, 8192], P(None, 'vocab'), may hold values from -3 to 3
Outputs:
- weight_grad: float32 [8192, 8192], P('dp', 'vocab')
- mean_loss: float32 [], replicated
Inputs may be any that keep to these rules, and one draw needn't show every extreme that they name: `exit_layers`: each row of 64 tokens names 2 different layers, and every layer is named by some row.
All inputs are finite; a program needn't handle non-finite values.
Results may differ from a plain program's by a relative error of at most 0.013.
Values may be sent and summed in bfloat16 or wider, within the bound.
A program may use at most 128 MiB of HBM per device.

v0:
```python
import jax
import jax.numpy as jnp
from jax import lax
from jax.sharding import PartitionSpec as P

norm_eps = 1e-05


def per_device(hidden_states, exit_layers, targets, norm_gain, exit_scale, unembedding):
    layers, tok_count, local_width = hidden_states.shape
    exit_count = exit_layers.shape[1]
    row_len = tok_count // exit_layers.shape[0]
    vocab_local = unembedding.shape[1]
    row_layers = jnp.repeat(exit_layers, row_len, axis=0)
    layer_match = row_layers.T[:, None, :] == jnp.arange(layers, dtype=jnp.int32)[None, :, None]
    selected = jnp.sum(
        jnp.where(layer_match[..., None], hidden_states[None].astype(jnp.float32), 0.0), axis=1
    ).astype(jnp.bfloat16)
    full_width = local_width * lax.axis_size("vocab")
    gain_values = norm_gain.astype(jnp.float32)
    gathered = lax.all_gather(selected, "vocab", axis=2, tiled=True)
    values = gathered.astype(jnp.float32)
    mean_sq = jnp.mean(values * values, axis=-1, keepdims=True)
    normed = (values * lax.rsqrt(mean_sq + norm_eps) * gain_values).astype(jnp.bfloat16)
    flat_normed = normed.reshape(exit_count * tok_count, full_width)
    logits = jnp.dot(flat_normed, unembedding, preferred_element_type=jnp.float32)
    target_rows = jnp.tile(targets, exit_count)
    vocab_ids = lax.axis_index("vocab") * vocab_local + jnp.arange(vocab_local, dtype=jnp.int32)
    is_target = target_rows[:, None] == vocab_ids[None, :]
    local_target = jnp.sum(jnp.where(is_target, logits, 0.0), axis=-1)
    local_max = jnp.max(logits, axis=-1)
    row_top = lax.pmax(local_max, "vocab")
    local_sum = jnp.sum(jnp.exp(logits - row_top[:, None]), axis=-1)
    exp_total, target_logit = lax.psum((local_sum, local_target), "vocab")
    log_total = row_top + jnp.log(exp_total)
    token_loss = log_total - target_logit
    scale_rows = jnp.repeat(exit_scale, tok_count)
    loss_sum = lax.psum(jnp.sum(scale_rows * token_loss), "dp")
    mean_loss = loss_sum / (tok_count * lax.axis_size("dp"))
    logit_grad = (
        scale_rows[:, None] * (jnp.exp(logits - log_total[:, None]) - is_target.astype(jnp.float32))
    ).astype(jnp.bfloat16)
    weight_grad = lax.psum_scatter(
        lax.dot_general(
            flat_normed, logit_grad, (((0,), (0,)), ((), ())), preferred_element_type=jnp.float32
        ).astype(jnp.bfloat16),
        "dp",
        scatter_dimension=0,
        tiled=True,
    ).astype(jnp.float32)
    return (weight_grad, mean_loss)


def solution(mesh):
    in_specs = (P(None, "dp", "vocab"), P("dp", None), P("dp"), P(), P(), P(None, "vocab"))
    out_specs = (P("dp", "vocab"), P())
    return jax.shard_map(
        per_device, mesh=mesh, in_specs=in_specs, out_specs=out_specs, check_vma=False
    )
```

profile of v0, /device:TPU:1, one launch (start us, length us, event | category | flops | bytes accessed | tf_op | source)
XLA Modules:
  0.0 481.8 jit_solution(3111374070935727855)
XLA Ops:
  7.2 0.0 copy-start
  7.2 0.0 all-gather.2.cloned.1.call-start
  7.2 1.1 convert_element_type.28
  8.4 0.8 broadcast_in_dim.39
  9.1 0.1 reshape.36
  9.2 1.2 select_reduce_fusion
  10.4 0.0 all-gather.2.cloned.1.call-update
  10.4 0.0 reduce-scatter.2.cloned.1.call-start
  10.5 0.7 convert_element_type.31
  11.2 0.0 copy-done
  11.2 0.7 broadcast_bitcast_fusion.1
  11.9 206.5 %all-gather.2.cloned.1.call-done = bf16[2,256,8192]{2,1,0:T(8,128)(2,1)} async-done(((bf16[2,256,256]{2,1,0:T(8,128)(2,1)}), bf16[2,256,8192]{2,1,0:T(8,128)(2,1)}) %all-gather.2.cloned.1.call-update) | async-done | bytes 8388624 | tf_op jit(solution)/shard_map/all_gather | solution.py:21
  218.4 5.1 %fusion = f32[2,256]{1,0:T(2,128)S(1)} fusion(bf16[2,256,8192]{2,1,0:T(8,128)(2,1)} %all-gather.2.cloned.1.call-done), kind=kLoop, calls=%fused_computation.2 | loop fusion | flops 12582400 | bytes 8390656 | tf_op jit(solution)/shard_map/reduce_sum | solution.py:23
  223.5 9.9 %fusion.2 = bf16[2,256,8192]{2,1,0:T(8,128)(2,1)} fusion(bf16[2,256,8192]{2,1,0:T(8,128)(2,1)} %all-gather.2.cloned.1.call-done, f32[8192]{0:T(1024)S(1)} %convert_element_type.31, f32[2,256]{1,0:T(2,128)S(1)} %add_rsqrt_fusion), kind=kLoop, calls=%fused_computation.4 | loop fusion | flops 16777216 | bytes 16812032 | tf_op jit(solution)/shard_map/convert_element_type | solution.py:24
  233.4 7.0 %fusion.12 = (f32[512]{0:T(512)S(1)}, f32[512,256]{0,1:T(8,128)S(1)}) fusion(bf16[512,8192]{1,0:T(8,128)(2,1)} %bitcast.13, bf16[8192,256]{1,0:T(8,128)(2,1)} %param.11), kind=kOutput, calls=%fused_computation.25 | convolution fusion | flops 2147614208 | bytes 13109248 | tf_op jit(solution)/shard_map/dot_general | solution.py:26
  240.3 60.5 %pmax.7 = f32[512]{0:T(512)S(1)} all-reduce(f32[512]{0:T(512)S(1)} %get-tuple-element.8), channel_id=1, replica_groups=mesh['dp'=16,'vocab'=32] {'vocab'}, use_global_device_ids=true, to_apply=%region_3.4 | all-reduce | flops 512 | bytes 4096 | tf_op jit(solution)/shard_map/pmax | solution.py:32
  300.8 0.1 fusion.6
  301.0 58.5 %all-reduce = (f32[512]{0:T(512)S(1)}, f32[512]{0:T(512)S(1)}) all-reduce(f32[512]{0:T(512)S(1)} %get-tuple-element.3, f32[512]{0:T(512)S(1)} %get-tuple-element.2), channel_id=1, replica_groups=mesh['dp'=16,'vocab'=32] {'vocab'}, use_global_device_ids=true, to_apply=%region_5.6 | all-reduce | flops 1024 | bytes 8192 | tf_op jit(solution)/shard_map/psum | solution.py:34
  359.4 0.6 multiply_reduce_fusion
  360.1 7.9 %convolution_convert_fusion = bf16[8192,256]{1,0:T(8,128)(2,1)} fusion(bf16[512,8192]{1,0:T(8,128)(2,1)} %bitcast.14, f32[512,256]{0,1:T(8,128)S(1)} %get-tuple-element.9, s32[512]{0:T(512)S(1)} %bitcast.16, f32[512]{0:T(512)S(1)} %get-tuple-element.7, f32[512]{0:T(512)S(1)} %bitcast.19, s32[256]{0:T(256)S(1)} %iota_add_fusion), kind=kOutput, calls=%fused_computation.5 | convolution fusion | flops 2150367232 | bytes 13114368 | tf_op jit(solution)/shard_map/dot_general | solution.py:44
  367.9 0.0 reduce-scatter.2.cloned.1.call-update
  367.9 64.6 %psum.23 = f32[]{:T(128)} all-reduce(f32[]{:T(128)} %get-tuple-element.6), channel_id=1, replica_groups=mesh['dp'=16,'vocab'=32] {'dp'}, use_global_device_ids=true, to_apply=%region_10.11 | all-reduce | flops 1 | bytes 8 | tf_op jit(solution)/shard_map/psum | solution.py:38
  433.2 38.9 %reduce-scatter.2.cloned.1.call-done = bf16[512,256]{1,0:T(8,128)(2,1)} async-done(((bf16[8192,256]{1,0:T(8,128)(2,1)}), bf16[512,256]{1,0:T(8,128)(2,1)}) %reduce-scatter.2.cloned.1.call-update) | async-done | bytes 262160 | tf_op jit(solution)/shard_map/reduce_scatter | solution.py:43
  472.1 1.8 convert_element_type.36
  (6 shorter events, 0.0 us)
Async XLA Ops:
  7.2 4.0 copy-start
  7.2 211.2 %all-gather.2.cloned.1.call-start = ((), (), s32[]{:S(2)}) async-start(), calls=%async_computation.1 | async-start | bytes 8650752 | tf_op jit(solution)/shard_map/all_gather | solution.py:21
  10.4 461.6 %reduce-scatter.2.cloned.1.call-start = ((), (), s32[]{:S(2)}) async-start(), calls=%async_computation.2 | async-start | bytes 4456448 | tf_op jit(solution)/shard_map/reduce_scatter | solution.py:43
Sparse Core Ops, SparseCore 0:
  11.5 206.8 all-gather.1
  368.1 103.9 reduce-scatter.1
where the time goes:
time: 483 us; the launch traced here: 482 us
  waiting for transfers between devices  245 us (51%)
  blocking collectives  184 us (38%)
  other arithmetic  20.5 us (4%)
  between operations  15.9 us (3%)
  matrix products  14.8 us (3%)
    all_gather x1, waiting for transfers between devices, per_device(): gathered = lax.all_gather(selected, 'vocab', axis=2, tiled=True)  206 us
    psum x1, blocking collectives, per_device(): loss_sum = lax.psum(jnp.sum(scale_rows * token_loss), 'dp')  64.6 us
    pmax x1, blocking collectives, per_device(): row_top = lax.pmax(local_max, 'vocab')  60.5 us
    psum x1, blocking collectives, per_device(): exp_total, target_logit = lax.psum((local_sum, local_target), 'vocab')  58.5 us
    reduce_scatter x1, waiting for transfers between devices, per_device(): lax.psum_scatter(lax.dot_general(flat_normed, logit_grad, (((0,), (0,)),...  38.9 us
    convert_element_type x1, other arithmetic, per_device(): (values * lax.rsqrt(mean_sq + norm_eps) * gain_values).astype(jnp.bfloat16)  9.85 us
  transfers between devices with their start and end apart: 2, of which 2 were waited for; matrix products, arithmetic and copies ran while one was open for 0% of the time, Pallas kernels for 0%

commit v1 on v0

v1 whole, which is shorter than its diff:
```python
import jax
import jax.numpy as jnp
from jax import lax
from jax.experimental import pallas as pl
from jax.experimental.pallas import tpu as pltpu
from jax.sharding import PartitionSpec as P

norm_eps = 1e-05
MESH = pl.DeviceIdType.MESH
F32 = jnp.float32
BF16 = jnp.bfloat16
NZ, NX, NY = 16, 4, 4


def kernel(x_ref, u_ref, tgt_ref, scale_ref, gain_ref, o_ref, loss_ref,
           abuf, ubuf, acc, ssq, gbuf, tbuf, sta, stb, zst, lebuf, lbuf, pbuf, fin,
           r_o, r_d, r_c, q_o, q_d, q_c,
           swap_sem, ring_s, ring_r, sib_s, sib_r, u_s, u_r, u_loc, t_sem, st_sem, z_s, z_r, le_sem,
           g_sem, l_s, l_r, rs_s, rs_r, qs_s, qs_r):
    dp = lax.axis_index("dp")
    vo = lax.axis_index("vocab")
    c = dp % 2
    xl = (dp // 2) % 2
    y = dp // 4
    z = vo % NZ
    xh = vo // NZ
    x = xh * 2 + xl

    def dev(x_, y_, z_, c_):
        return ((y_ * 2 + x_ % 2) * 2 + c_, (x_ // 2) * NZ + z_)

    sibling = dev(x, y, z, 1 - c)
    partner = dev((x + 2) % 4, y, z, 1 - c)

    def rcopy(src, dst, s, r, to):
        return pltpu.make_async_remote_copy(src_ref=src, dst_ref=dst, send_sem=s, recv_sem=r,
                                            device_id=to, device_id_type=MESH)

    bar = pltpu.get_barrier_semaphore()

    def hello(to):
        pl.semaphore_signal(bar, inc=1, device_id=to, device_id_type=MESH)

    hello(sibling)
    hello(partner)

    def hello_z(k, carry):
        hello(dev(x, y, (z + k) % NZ, c))
        hello(dev((x + k % 4) % 4, (y + k // 4) % 4, z, c))
        return carry

    lax.fori_loop(1, 16, hello_z, 0)
    pl.semaphore_wait(bar, 32)

    mine = c == xh
    swap = rcopy(x_ref, abuf.at[1 - c, z], swap_sem.at[0], swap_sem.at[1], partner)
    swap_in = rcopy(x_ref, abuf.at[c, z], swap_sem.at[0], swap_sem.at[1], partner)

    def u_direct(k):
        j = (1 - xl) * 8 + k
        return rcopy(u_ref.at[pl.ds(2 * j, 2)], ubuf.at[pl.ds(2 * j, 2)], u_s.at[0, k], u_r.at[0, k], dev(3 - x, y, z, c))

    def u_direct_in(k):
        j = xl * 8 + k
        return rcopy(ubuf.at[pl.ds(2 * j, 2)], ubuf.at[pl.ds(2 * j, 2)], u_s.at[0, k], u_r.at[0, k], dev(3 - x, y, z, c))

    def u_mate(k):
        j = xl * 8 + k
        return rcopy(ubuf.at[pl.ds(2 * j, 2)], ubuf.at[pl.ds(2 * j, 2)], u_s.at[1, k], u_r.at[1, k], dev(xh * 2 + 1 - xl, y, z, c))

    def u_mate_in(k):
        j = (1 - xl) * 8 + k
        return rcopy(ubuf.at[pl.ds(2 * j, 2)], ubuf.at[pl.ds(2 * j, 2)], u_s.at[1, k], u_r.at[1, k], dev(xh * 2 + 1 - xl, y, z, c))

    u_local = pltpu.make_async_copy(u_ref, ubuf, u_loc)

    @pl.when(jnp.logical_not(mine))
    def _():
        swap.start()

    t_copy = rcopy(tgt_ref, tbuf, t_sem.at[0], t_sem.at[1], sibling)
    t_copy.start()

    @pl.when(mine)
    def _():
        abuf[c, z] = x_ref[...]
        u_local.start()

        def send_u(k, carry):
            u_direct(k).start()
            return carry

        lax.fori_loop(0, 8, send_u, 0)

    @pl.when(jnp.logical_not(mine))
    def _():
        swap_in.wait_recv()

    def step_slot(d, i):
        return (z - i + NZ) % NZ if d == 0 else (z + i) % NZ

    def half(slot, h):
        return abuf.at[c, slot, pl.ds(256 * h, 256)]

    def ring(d, h, i):
        ref = half(step_slot(d, i - 1), h)
        to = dev(x, y, (z + 1) % NZ, c) if d == 0 else dev(x, y, (z + NZ - 1) % NZ, c)
        return rcopy(ref, ref, ring_s.at[d, h, i - 1], ring_r.at[d, h, i - 1], to)

    def ring_in(d, h, i):
        ref = half(step_slot(d, i), h)
        to = dev(x, y, (z + 1) % NZ, c) if d == 0 else dev(x, y, (z + NZ - 1) % NZ, c)
        return rcopy(ref, ref, ring_s.at[d, h, i - 1], ring_r.at[d, h, i - 1], to)

    def sib(n, slot, h):
        ref = half(slot, h)
        return rcopy(ref, ref, sib_s.at[n, h], sib_r.at[n, h], sibling)

    def sib_in(n, slot, h):
        ref = abuf.at[1 - c, slot, pl.ds(256 * h, 256)]
        return rcopy(ref, ref, sib_s.at[n, h], sib_r.at[n, h], sibling)

    for h in range(2):
        for d in range(2):
            ring(d, h, 1).start()
    for h in range(2):
        sib(0, z, h).start()

    acc[...] = jnp.zeros_like(acc)
    ssq[...] = jnp.zeros_like(ssq)

    def ring_step(i, more):
        for h in range(2):
            for d in range(2):
                ring_in(d, h, i).wait_recv()
                if more == 2 or (more == 1 and h == d):
                    ring(d, h, i + 1).start()
                sib(2 * i - d, step_slot(d, i), h).start()

    def block_slot(n):
        off = jnp.where(n % 2 == 1, (n + 1) // 2, NZ - n // 2)
        return (z + off) % NZ

    def blocks(n, carry):
        slot = block_slot(n)
        for h in range(2):
            sib_in(n, slot, h).wait_recv()
        for cs in range(2):
            s = cs * NZ + slot
            a = abuf[cs, slot].astype(F32)
            ssq[...] += a[:, :128] * a[:, :128] + a[:, 128:] * a[:, 128:]
            ag = (a * gain_ref[pl.ds(s, 1), :]).astype(BF16)
            acc[...] += lax.dot_general(ubuf[s], ag, (((0,), (1,)), ((), ())), preferred_element_type=F32)
        return carry

    def loop_step(i, carry):
        ring_step(i, 2)

        @pl.when(jnp.logical_not(mine))
        def _():
            for k in range(2):
                u_direct_in(2 * (i - 1) + k).wait_recv()
                u_mate(2 * (i - 1) + k).start()
        return carry

    lax.fori_loop(1, 5, loop_step, 0)
    ring_step(5, 2)

    @pl.when(jnp.logical_not(mine))
    def _():
        def wait_u(k, carry):
            u_mate_in(k).wait_recv()
            return carry

        lax.fori_loop(0, 8, wait_u, 0)

    @pl.when(mine)
    def _():
        u_local.wait()

    lax.fori_loop(0, 5, blocks, 0)
    ring_step(6, 2)
    lax.fori_loop(5, 10, blocks, 0)
    ring_step(7, 1)
    lax.fori_loop(10, 13, blocks, 0)
    for d in range(2):
        ring_in(d, d, 8).wait_recv()
        sib(15, (z + 8) % NZ, d).start()
    lax.fori_loop(13, 16, blocks, 0)

    mean_sq = jnp.sum(ssq[...].T, axis=0, keepdims=True) * (1.0 / 8192.0)
    r_row = lax.rsqrt(mean_sq + norm_eps)
    logits = acc[...] * r_row
    acc[...] = logits
    t_copy.wait_recv()
    tgt = jnp.where(mine, tgt_ref[0:1, :], tbuf[0:1, :])
    ids = (((c * NZ + z) * 256) + lax.broadcasted_iota(jnp.int32, (256, 512), 0)).astype(F32)
    is_target = ids == tgt
    m = jnp.max(logits, axis=0, keepdims=True)
    sta[0:1, :] = m
    sta[1:2, :] = jnp.sum(jnp.exp(logits - m), axis=0, keepdims=True)
    sta[2:3, :] = jnp.sum(jnp.where(is_target, logits, 0.0), axis=0, keepdims=True)
    st_copy = rcopy(sta, stb, st_sem.at[0], st_sem.at[1], sibling)
    st_copy.start()
    st_copy.wait_recv()
    cols = pl.ds(pl.multiple_of(c * 256, 256), 256)
    m_a, m_b = sta[0:1, cols], stb[0:1, cols]
    m2 = jnp.maximum(m_a, m_b)
    s2 = sta[1:2, cols] * jnp.exp(m_a - m2) + stb[1:2, cols] * jnp.exp(m_b - m2)
    t2 = sta[2:3, cols] + stb[2:3, cols]
    zst[z] = jnp.concatenate(
        [m2[:, :128], m2[:, 128:], s2[:, :128], s2[:, 128:], t2[:, :128], t2[:, 128:], t2[:, :128], t2[:, 128:]], axis=0)

    def z_copy(k):
        return rcopy(zst.at[z], zst.at[z], z_s.at[k], z_r.at[k], dev(x, y, (z + k) % NZ, c))

    def z_in(k):
        slot = (z + NZ - k) % NZ
        return rcopy(zst.at[slot], zst.at[slot], z_s.at[k], z_r.at[k], dev(x, y, (z + k) % NZ, c))

    def z_start(k, carry):
        z_copy(k).start()
        return carry

    def z_wait(k, carry):
        z_in(k).wait_recv()
        return carry

    lax.fori_loop(1, NZ, z_start, 0)
    lax.fori_loop(1, NZ, z_wait, 0)
    st = zst[...]
    m16, s16, t16 = st[:, 0:2, :], st[:, 2:4, :], st[:, 4:6, :]
    top = jnp.max(m16, axis=0)
    lse = top + jnp.log(jnp.sum(s16 * jnp.exp(m16 - top[None]), axis=0))
    t_all = jnp.sum(t16, axis=0)
    lebuf[c] = jnp.concatenate([lse, t_all, lse, t_all], axis=0)
    le_copy = rcopy(lebuf.at[c], lebuf.at[c], le_sem.at[0], le_sem.at[1], sibling)
    le_in = rcopy(lebuf.at[1 - c], lebuf.at[1 - c], le_sem.at[0], le_sem.at[1], sibling)
    le_copy.start()
    le_in.wait_recv()
    lse_row = jnp.concatenate([lebuf[0, 0:1, :], lebuf[0, 1:2, :], lebuf[1, 0:1, :], lebuf[1, 1:2, :]], axis=1)
    t_row = jnp.concatenate([lebuf[0, 2:3, :], lebuf[0, 3:4, :], lebuf[1, 2:3, :], lebuf[1, 3:4, :]], axis=1)
    scale_row = scale_ref[0:1, :]
    grad = (scale_row * r_row) * (jnp.exp(acc[...] - lse_row) - is_target.astype(F32))
    gbuf[c] = grad.astype(BF16)
    g_copy = rcopy(gbuf.at[c], gbuf.at[c], g_sem.at[0], g_sem.at[1], sibling)
    g_in = rcopy(gbuf.at[1 - c], gbuf.at[1 - c], g_sem.at[0], g_sem.at[1], sibling)
    g_copy.start()

    loss4 = scale_row * (lse_row - t_row)
    loss1 = loss4[:, :128] + loss4[:, 128:256] + loss4[:, 256:384] + loss4[:, 384:]
    me = y * 4 + x
    lbuf[me] = jnp.broadcast_to(loss1, (8, 128))

    def l_copy(k):
        return rcopy(lbuf.at[me], lbuf.at[me], l_s.at[k], l_r.at[k], dev((x + k % 4) % 4, (y + k // 4) % 4, z, c))

    def l_in(k):
        slot = (y + 4 - k // 4) % 4 * 4 + (x + 4 - k % 4) % 4
        return rcopy(lbuf.at[slot], lbuf.at[slot], l_s.at[k], l_r.at[k], dev((x + k % 4) % 4, (y + k // 4) % 4, z, c))

    def l_start(k, carry):
        l_copy(k).start()
        return carry

    def l_wait(k, carry):
        l_in(k).wait_recv()
        l_copy(k).wait_send()
        return carry

    g_in.wait_recv()

    def along(axis, step):
        if axis == 0:
            return dev((x + step) % 4, y, z, c)
        return dev(x, (y + step) % 4, z, c)

    def grad_block(dy, dx):
        y_, x_ = (y + dy) % 4, (x + dx) % 4
        s = ((y_ * 2 + x_ % 2) * 2 + c) * 2
        plane, slot = s // NZ, s % NZ
        for k in range(2):
            pbuf[y_, x_, :, 256 * k:256 * k + 256] = jnp.dot(
                gbuf[x_ // 2], abuf[plane, slot + k], preferred_element_type=F32).astype(BF16)

    def blk(axis, step, o):
        if axis == 0:
            return pbuf.at[(y + o) % 4, (x + step) % 4]
        return pbuf.at[(y + step) % 4, (x + o) % 4]

    def part(axis, which):
        return pl.ds(128 * axis + 64 * which, 64)

    STEP = (1, 3)

    def send_o(axis, d, o):
        return rcopy(blk(axis, 2, o).at[part(axis, d)], r_o.at[axis, d, o], rs_s.at[0, axis, d, o], rs_r.at[0, axis, d, o], along(axis, STEP[d]))

    def send_d(axis, d, o):
        return rcopy(blk(axis, STEP[d], o).at[part(axis, 1 - d)], r_d.at[axis, d, o], rs_s.at[1, axis, d, o], rs_r.at[1, axis, d, o], along(axis, STEP[d]))

    def send_c(axis, d, o):
        return rcopy(blk(axis, STEP[d], o).at[part(axis, d)], r_c.at[axis, d, o], rs_s.at[2, axis, d, o], rs_r.at[2, axis, d, o], along(axis, STEP[d]))

    def send_o2(axis, d):
        return rcopy(blk(axis, 0, 2).at[part(axis, d)], q_o.at[axis, d], qs_s.at[0, axis, d], qs_r.at[0, axis, d], along(1 - axis, STEP[d]))

    def send_d2(axis, d):
        return rcopy(blk(axis, 0, STEP[d]).at[part(axis, 1 - d)], q_d.at[axis, d], qs_s.at[1, axis, d], qs_r.at[1, axis, d], along(1 - axis, STEP[d]))

    def send_c2(axis, d):
        return rcopy(blk(axis, 0, STEP[d]).at[part(axis, d)], q_c.at[axis, d], qs_s.at[2, axis, d], qs_r.at[2, axis, d], along(1 - axis, STEP[d]))

    def start_o(axis, o):
        for d in range(2):
            send_o(axis, d, o).start()

    def start_d(axis, o):
        for d in range(2):
            send_d(axis, d, o).start()

    ORDER = (2, 1, 3, 0)
    grad_block(2, 2)
    start_o(0, 2)
    start_o(1, 2)

    def o_blocks(k, carry):
        o = k
        grad_block(o, 2)
        start_o(0, o)
        grad_block(2, o)
        start_o(1, o)
        return carry

    o_blocks(1, 0)
    o_blocks(3, 0)
    o_blocks(0, 0)
    start_d(0, 2)
    start_d(1, 2)
    for dy in (1, 3):
        for dx in (1, 3):
            grad_block(dy, dx)
    for o in (1, 3):
        start_d(0, o)
        start_d(1, o)
    for dd in (1, 3):
        grad_block(0, dd)
        grad_block(dd, 0)
    start_d(0, 0)
    start_d(1, 0)
    grad_block(0, 0)
    lax.fori_loop(1, 16, l_start, 0)

    for o in ORDER:
        for axis in range(2):
            for d in range(2):
                send_o(axis, d, o).wait_recv()
                ref = blk(axis, STEP[d], o)
                rows = part(axis, d)
                ref[rows, :] = (ref[rows, :].astype(F32) + r_o[axis, d, o].astype(F32)).astype(BF16)
                send_c(axis, d, o).start()

    for o in ORDER:
        for axis in range(2):
            own = blk(axis, 0, o)
            for w in range(2):
                send_c(axis, w, o).wait_recv()
                send_d(axis, 1 - w, o).wait_recv()
                rows = part(axis, w)
                total = own[rows, :].astype(F32) + r_c[axis, w, o].astype(F32) + r_d[axis, 1 - w, o].astype(F32)
                if o == 0:
                    fin[rows, :] = total
                else:
                    own[rows, :] = total.astype(BF16)
            if o == 2:
                for d in range(2):
                    send_o2(axis, d).start()
            if o in STEP:
                send_d2(axis, STEP.index(o)).start()

    for axis in range(2):
        for d in range(2):
            send_o2(axis, d).wait_recv()
            ref = blk(axis, 0, STEP[d])
            rows = part(axis, d)
            ref[rows, :] = (ref[rows, :].astype(F32) + q_o[axis, d].astype(F32)).astype(BF16)
            send_c2(axis, d).start()

    s_own = ((y * 2 + xl) * 2 + c) * 2
    gain_own = jnp.concatenate([gain_ref[pl.ds(s_own, 1), :], gain_ref[pl.ds(s_own + 1, 1), :]], axis=1)
    for axis in range(2):
        for w in range(2):
            send_c2(axis, w).wait_recv()
            send_d2(axis, 1 - w).wait_recv()
            rows = part(axis, w)
            o_ref[rows, :] = (fin[rows, :] + q_c[axis, w].astype(F32) + q_d[axis, 1 - w].astype(F32)) * gain_own

    lax.fori_loop(1, 16, l_wait, 0)
    tot = jnp.sum(lbuf[...], axis=0)
    loss_ref[...] = jnp.broadcast_to(jnp.sum(tot, axis=1, keepdims=True) * (1.0 / 4096.0), (8, 128))

    for axis in range(2):
        for d in range(2):
            for o in range(4):
                send_o(axis, d, o).wait_send()
                send_d(axis, d, o).wait_send()
                send_c(axis, d, o).wait_send()
            send_o2(axis, d).wait_send()
            send_d2(axis, d).wait_send()
            send_c2(axis, d).wait_send()
    for copy in (t_copy, st_copy, le_copy, g_copy):
        copy.wait_send()

    def z_done(k, carry):
        z_copy(k).wait_send()
        return carry

    lax.fori_loop(1, NZ, z_done, 0)

    def ring_done(i, carry):
        for h in range(2):
            for d in range(2):
                ring(d, h, i).wait_send()
        return carry

    lax.fori_loop(1, 8, ring_done, 0)
    for d in range(2):
        ring(d, d, 8).wait_send()

    def sib_done(n, carry):
        for h in range(2):
            sib(n, block_slot(n), h).wait_send()
        return carry

    lax.fori_loop(0, 16, sib_done, 0)

    @pl.when(mine)
    def _():
        def done(k, carry):
            u_direct(k).wait_send()
            return carry

        lax.fori_loop(0, 8, done, 0)

    @pl.when(jnp.logical_not(mine))
    def _():
        swap.wait_send()

        def done(k, carry):
            u_mate(k).wait_send()
            return carry

        lax.fori_loop(0, 8, done, 0)


def per_device(hidden_states, exit_layers, targets, norm_gain, exit_scale, unembedding):
    layers, tok_count, local_width = hidden_states.shape
    exit_count = exit_layers.shape[1]
    row_len = tok_count // exit_layers.shape[0]
    row_layers = jnp.repeat(exit_layers, row_len, axis=0)
    layer_match = row_layers.T[:, None, :] == jnp.arange(layers, dtype=jnp.int32)[None, :, None]
    selected = jnp.sum(
        jnp.where(layer_match[..., None], hidden_states[None].astype(F32), 0.0), axis=1
    ).astype(BF16).reshape(exit_count * tok_count, local_width)
    tgt = jnp.broadcast_to(jnp.tile(targets, exit_count).astype(F32)[None], (8, 512))
    scale = jnp.broadcast_to(jnp.repeat(exit_scale, tok_count)[None], (8, 512))
    gain = norm_gain.astype(F32).reshape(32, 256)
    vmem = pl.BlockSpec(memory_space=pltpu.VMEM)
    dma = pltpu.SemaphoreType.DMA
    grad_t, loss = pl.pallas_call(
        kernel,
        out_shape=(jax.ShapeDtypeStruct((256, 512), F32), jax.ShapeDtypeStruct((8, 128), F32)),
        in_specs=[vmem, pl.BlockSpec(memory_space=pl.ANY), vmem, vmem, vmem],
        out_specs=(vmem, vmem),
        scratch_shapes=[
            pltpu.VMEM((2, 16, 512, 256), BF16),
            pltpu.VMEM((32, 256, 256), BF16),
            pltpu.VMEM((256, 512), F32),
            pltpu.VMEM((512, 128), F32),
            pltpu.VMEM((2, 256, 512), BF16),
            pltpu.VMEM((8, 512), F32),
            pltpu.VMEM((8, 512), F32),
            pltpu.VMEM((8, 512), F32),
            pltpu.VMEM((16, 8, 128), F32),
            pltpu.VMEM((2, 8, 128), F32),
            pltpu.VMEM((16, 8, 128), F32),
            pltpu.VMEM((4, 4, 256, 512), BF16),
            pltpu.VMEM((256, 512), F32),
            pltpu.VMEM((2, 2, 4, 64, 512), BF16),
            pltpu.VMEM((2, 2, 4, 64, 512), BF16),
            pltpu.VMEM((2, 2, 4, 64, 512), BF16),
            pltpu.VMEM((2, 2, 64, 512), BF16),
            pltpu.VMEM((2, 2, 64, 512), BF16),
            pltpu.VMEM((2, 2, 64, 512), BF16),
            dma((2,)), dma((2, 2, 8)), dma((2, 2, 8)), dma((16, 2)), dma((16, 2)),
            dma((2, 8)), dma((2, 8)), dma, dma((2,)), dma((2,)), dma((16,)), dma((16,)), dma((2,)),
            dma((2,)), dma((16,)), dma((16,)), dma((3, 2, 2, 4)), dma((3, 2, 2, 4)), dma((3, 2, 2)), dma((3, 2, 2)),
        ],
        compiler_params=pltpu.CompilerParams(
            collective_id=0, has_side_effects=True, vmem_limit_bytes=56 << 20),
    )(selected, unembedding.reshape(32, 256, 256), tgt, scale, gain)
    return (grad_t.T, loss[0, 0])


def solution(mesh):
    in_specs = (P(None, "dp", "vocab"), P("dp", None), P("dp"), P(), P(), P(None, "vocab"))
    out_specs = (P("dp", "vocab"), P())
    return jax.shard_map(
        per_device, mesh=mesh, in_specs=in_specs, out_specs=out_specs, check_vma=False
    )
```

time: 483 us -> 120 us (0.25)
  the two profiles are of different devices: /device:TPU:1 before, /device:TPU:2 now
where the time goes in v1:
time: 120 us; the launch traced here: 119 us
  Pallas kernels  110 us (92%)
  local copies, waits for them, and re-layouts  5.97 us (5%)
  other arithmetic  2.35 us (2%)
    pallas_call x1, Pallas kernels, per_device(): pl.pallas_call(kernel, out_shape=(jax.ShapeDtypeStruct((256, 512), F32),...  110 us

profile of v1, /device:TPU:2, one launch (start us, length us, event | category | flops | bytes accessed | tf_op | source)
XLA Modules:
  0.0 119.3 jit_solution(12205592222725440936)
XLA Ops:
  0.6 0.0 copy-start
  0.6 0.0 copy-start.1
  0.7 0.0 copy-start.2
  0.7 1.1 convert_element_type.23
  1.8 0.8 broadcast_in_dim.43
  2.6 0.1 reshape.33
  2.7 1.2 %select_reduce_fusion = bf16[2,256,256]{2,1,0:T(8,128)(2,1)} fusion(f32[4,256,256]{2,1,0:T(8,128)S(1)} %convert_element_type.23, pred[2,4,256]{2,1,0:T(4,128)(4,1)S(1)} %iota_compare_fusion), kind=kLoop, calls=%fused_computation | loop fusion | flops 917504 | bytes 1312768 | tf_op jit(solution)/shard_map/reduce_sum | solution.py:462
  3.9 0.0 copy-done.1
  3.9 0.6 reshape.38.gain_ref
  4.5 0.0 copy-done.2
  4.5 0.6 broadcast_in_dim.47.tgt_ref
  5.1 0.0 copy-done
  5.1 0.1 broadcast_bitcast_fusion.1
  5.2 0.6 broadcast_in_dim.50.scale_ref
  5.8 110.3 %shard_map.77 = (f32[256,512]{1,0:T(8,128)}, f32[8,128]{1,0:T(8,128)}) custom-call(bf16[512,256]{1,0:T(8,128)(2,1)} %bitcast.14, bf16[32,256,256]{2,1,0:T(8,128)(2,1)} %bitcast.13, f32[8,512]{1,0:T(8,128)} %broadcast_in_dim.47.tgt_ref, f32[8,512]{1,0:T(8,128)} %broadcast_in_dim.50.scale_ref, f32[32,256]{1,0:T(8,128)} %reshape.38.gain_ref), custom_call_target="tpu_custom_call" | custom-call | tf_op jit(solution)/shard_map/pallas_call | solution.py:470
  116.1 2.0 %copy.11 = f32[512,256]{1,0:T(8,128)} copy(f32[512,256]{0,1:T(8,128)} %bitcast.15) | data formatting | bytes 1048576
  118.1 1.2 slice.3
  (5 shorter events, 0.0 us)
Async XLA Ops:
  0.6 4.5 %copy-start = (f32[2]{0:T(128)S(1)}, f32[2]{0:T(128)}, u32[]{:S(2)}) copy-start(f32[2]{0:T(128)} %param.10) | copy-start | bytes 28
  0.6 3.2 %copy-start.1 = (bf16[8192]{0:T(1024)(128)(2,1)S(1)}, bf16[8192]{0:T(1024)(128)(2,1)}, u32[]{:S(2)}) copy-start(bf16[8192]{0:T(1024)(128)(2,1)} %param.9) | copy-start | bytes 49156
  0.7 3.8 %copy-start.2 = (s32[256]{0:T(256)S(1)}, s32[256]{0:T(256)}, u32[]{:S(2)}) copy-start(s32[256]{0:T(256)} %param.8) | copy-start | bytes 3076

commit v2 on v1

--- a/solution.py
+++ b/solution.py
@@ -12,8 +12,8 @@
 NZ, NX, NY = 16, 4, 4
 
 
-def kernel(x_ref, u_ref, tgt_ref, scale_ref, gain_ref, o_ref, loss_ref,
-           abuf, ubuf, acc, ssq, gbuf, tbuf, sta, stb, zst, lebuf, lbuf, pbuf, fin,
+def kernel(el_ref, scale_ref, hid_ref, u_ref, tgt_ref, gain_ref, o_ref, loss_ref,
+           hbuf, xbuf, tsrc, gain, in_sem, abuf, ubuf, acc, ssq, gbuf, tbuf, sta, stb, zst, lebuf, lbuf, pbuf, fin,
            r_o, r_d, r_c, q_o, q_d, q_c,
            swap_sem, ring_s, ring_r, sib_s, sib_r, u_s, u_r, u_loc, t_sem, st_sem, z_s, z_r, le_sem,
            g_sem, l_s, l_r, rs_s, rs_r, qs_s, qs_r):
@@ -36,6 +36,9 @@
         return pltpu.make_async_remote_copy(src_ref=src, dst_ref=dst, send_sem=s, recv_sem=r,
                                             device_id=to, device_id_type=MESH)
 
+    hid_copy = pltpu.make_async_copy(hid_ref, hbuf, in_sem)
+    hid_copy.start()
+
     bar = pltpu.get_barrier_semaphore()
 
     def hello(to):
@@ -50,11 +53,27 @@
         return carry
 
     lax.fori_loop(1, 16, hello_z, 0)
+
+    def select(dst):
+        for e in range(2):
+            for row in range(4):
+                dst[pl.ds(256 * e + 64 * row, 64), :] = hbuf[el_ref[e, row], pl.ds(64 * row, 64), :]
+
+    mine = c == xh
+    hid_copy.wait()
+
+    @pl.when(mine)
+    def _():
+        select(abuf.at[c, z])
+
+    @pl.when(jnp.logical_not(mine))
+    def _():
+        select(xbuf)
+
     pl.semaphore_wait(bar, 32)
 
-    mine = c == xh
-    swap = rcopy(x_ref, abuf.at[1 - c, z], swap_sem.at[0], swap_sem.at[1], partner)
-    swap_in = rcopy(x_ref, abuf.at[c, z], swap_sem.at[0], swap_sem.at[1], partner)
+    swap = rcopy(xbuf, abuf.at[1 - c, z], swap_sem.at[0], swap_sem.at[1], partner)
+    swap_in = rcopy(xbuf, abuf.at[c, z], swap_sem.at[0], swap_sem.at[1], partner)
 
     def u_direct(k):
         j = (1 - xl) * 8 + k
@@ -78,12 +97,12 @@
     def _():
         swap.start()
 
-    t_copy = rcopy(tgt_ref, tbuf, t_sem.at[0], t_sem.at[1], sibling)
+    tsrc[0:2, :] = tgt_ref[...].astype(F32)
+    t_copy = rcopy(tsrc, tbuf, t_sem.at[0], t_sem.at[1], sibling)
     t_copy.start()
 
     @pl.when(mine)
     def _():
-        abuf[c, z] = x_ref[...]
         u_local.start()
 
         def send_u(k, carry):
@@ -125,6 +144,11 @@
             ring(d, h, 1).start()
     for h in range(2):
         sib(0, z, h).start()
+
+    gain[...] = gain_ref[...].astype(F32)
+
+    def gain_row(s):
+        return jnp.concatenate([gain[pl.ds(2 * s, 1), :], gain[pl.ds(2 * s + 1, 1), :]], axis=1)
 
     acc[...] = jnp.zeros_like(acc)
     ssq[...] = jnp.zeros_like(ssq)
@@ -149,7 +173,7 @@
             s = cs * NZ + slot
             a = abuf[cs, slot].astype(F32)
             ssq[...] += a[:, :128] * a[:, :128] + a[:, 128:] * a[:, 128:]
-            ag = (a * gain_ref[pl.ds(s, 1), :]).astype(BF16)
+            ag = (a * gain_row(s)).astype(BF16)
             acc[...] += lax.dot_general(ubuf[s], ag, (((0,), (1,)), ((), ())), preferred_element_type=F32)
         return carry
 
@@ -193,7 +217,8 @@
     logits = acc[...] * r_row
     acc[...] = logits
     t_copy.wait_recv()
-    tgt = jnp.where(mine, tgt_ref[0:1, :], tbuf[0:1, :])
+    t2x = jnp.where(mine, tsrc[0:2, :], tbuf[0:2, :])
+    tgt = jnp.concatenate([t2x[0:1, :], t2x[1:2, :], t2x[0:1, :], t2x[1:2, :]], axis=1)
     ids = (((c * NZ + z) * 256) + lax.broadcasted_iota(jnp.int32, (256, 512), 0)).astype(F32)
     is_target = ids == tgt
     m = jnp.max(logits, axis=0, keepdims=True)
@@ -240,7 +265,7 @@
     le_in.wait_recv()
     lse_row = jnp.concatenate([lebuf[0, 0:1, :], lebuf[0, 1:2, :], lebuf[1, 0:1, :], lebuf[1, 1:2, :]], axis=1)
     t_row = jnp.concatenate([lebuf[0, 2:3, :], lebuf[0, 3:4, :], lebuf[1, 2:3, :], lebuf[1, 3:4, :]], axis=1)
-    scale_row = scale_ref[0:1, :]
+    scale_row = jnp.where(lax.broadcasted_iota(jnp.int32, (1, 512), 1) < 256, scale_ref[0], scale_ref[1])
     grad = (scale_row * r_row) * (jnp.exp(acc[...] - lse_row) - is_target.astype(F32))
     gbuf[c] = grad.astype(BF16)
     g_copy = rcopy(gbuf.at[c], gbuf.at[c], g_sem.at[0], g_sem.at[1], sibling)
@@ -387,7 +412,7 @@
             send_c2(axis, d).start()
 
     s_own = ((y * 2 + xl) * 2 + c) * 2
-    gain_own = jnp.concatenate([gain_ref[pl.ds(s_own, 1), :], gain_ref[pl.ds(s_own + 1, 1), :]], axis=1)
+    gain_own = jnp.concatenate([gain_row(s_own), gain_row(s_own + 1)], axis=1)
     for axis in range(2):
         for w in range(2):
             send_c2(axis, w).wait_recv()
@@ -397,7 +422,7 @@
 
     lax.fori_loop(1, 16, l_wait, 0)
     tot = jnp.sum(lbuf[...], axis=0)
-    loss_ref[...] = jnp.broadcast_to(jnp.sum(tot, axis=1, keepdims=True) * (1.0 / 4096.0), (8, 128))
+    loss_ref[0] = jnp.sum(tot[0:1, :]) * (1.0 / 4096.0)
 
     for axis in range(2):
         for d in range(2):
@@ -454,31 +479,27 @@
 
 
 def per_device(hidden_states, exit_layers, targets, norm_gain, exit_scale, unembedding):
-    layers, tok_count, local_width = hidden_states.shape
-    exit_count = exit_layers.shape[1]
-    row_len = tok_count // exit_layers.shape[0]
-    row_layers = jnp.repeat(exit_layers, row_len, axis=0)
-    layer_match = row_layers.T[:, None, :] == jnp.arange(layers, dtype=jnp.int32)[None, :, None]
-    selected = jnp.sum(
-        jnp.where(layer_match[..., None], hidden_states[None].astype(F32), 0.0), axis=1
-    ).astype(BF16).reshape(exit_count * tok_count, local_width)
-    tgt = jnp.broadcast_to(jnp.tile(targets, exit_count).astype(F32)[None], (8, 512))
-    scale = jnp.broadcast_to(jnp.repeat(exit_scale, tok_count)[None], (8, 512))
-    gain = norm_gain.astype(F32).reshape(32, 256)
     vmem = pl.BlockSpec(memory_space=pltpu.VMEM)
+    smem = pl.BlockSpec(memory_space=pltpu.SMEM)
+    anywhere = pl.BlockSpec(memory_space=pl.ANY)
     dma = pltpu.SemaphoreType.DMA
     grad_t, loss = pl.pallas_call(
         kernel,
-        out_shape=(jax.ShapeDtypeStruct((256, 512), F32), jax.ShapeDtypeStruct((8, 128), F32)),
-        in_specs=[vmem, pl.BlockSpec(memory_space=pl.ANY), vmem, vmem, vmem],
-        out_specs=(vmem, vmem),
+        out_shape=(jax.ShapeDtypeStruct((256, 512), F32), jax.ShapeDtypeStruct((1,), F32)),
+        in_specs=[smem, smem, anywhere, anywhere, vmem, vmem],
+        out_specs=(vmem, smem),
         scratch_shapes=[
+            pltpu.VMEM((4, 256, 256), BF16),
+            pltpu.VMEM((512, 256), BF16),
+            pltpu.VMEM((8, 128), F32),
+            pltpu.VMEM((64, 128), F32),
+            dma,
             pltpu.VMEM((2, 16, 512, 256), BF16),
             pltpu.VMEM((32, 256, 256), BF16),
             pltpu.VMEM((256, 512), F32),
             pltpu.VMEM((512, 128), F32),
             pltpu.VMEM((2, 256, 512), BF16),
-            pltpu.VMEM((8, 512), F32),
+            pltpu.VMEM((8, 128), F32),
             pltpu.VMEM((8, 512), F32),
             pltpu.VMEM((8, 512), F32),
             pltpu.VMEM((16, 8, 128), F32),
@@ -498,8 +519,9 @@
         ],
         compiler_params=pltpu.CompilerParams(
             collective_id=0, has_side_effects=True, vmem_limit_bytes=56 << 20),
-    )(selected, unembedding.reshape(32, 256, 256), tgt, scale, gain)
-    return (grad_t.T, loss[0, 0])
+    )(exit_layers.T, exit_scale, hidden_states, unembedding.reshape(32, 256, 256),
+      targets.reshape(2, 128), norm_gain.reshape(64, 128))
+    return (grad_t.T, loss.reshape(()))
 
 
 def solution(mesh):

time: 120 us -> 115 us (0.958)
  the two profiles are of different devices: /device:TPU:2 before, /device:TPU:1 now
where the time goes in v2:
time: 115 us; the launch traced here: 113 us
  Pallas kernels  108 us (94%)
  between operations  2.34 us (2%)
  local copies, waits for them, and re-layouts  2.04 us (2%)
    pallas_call x1, Pallas kernels, per_device(): pl.pallas_call(kernel, out_shape=(jax.ShapeDtypeStruct((256, 512), F32),...  108 us

profile of v2, /device:TPU:1, one launch (start us, length us, event | category | flops | bytes accessed | tf_op | source)
XLA Modules:
  0.0 112.8 jit_solution(17194828822096628773)
XLA Ops:
  0.6 108.4 %shard_map.77 = (f32[256,512]{1,0:T(8,128)}, f32[1]{0:T(128)}) custom-call(s32[2,4]{1,0:T(2,128)} %bitcast.9, f32[2]{0:T(128)} %scale_ref.1, bf16[4,256,256]{2,1,0:T(8,128)(2,1)} %hid_ref.1, bf16[32,256,256]{2,1,0:T(8,128)(2,1)} %bitcast.6, s32[2,128]{1,0:T(2,128)} %bitcast.10, bf16[64,128]{1,0:T(8,128)(2,1)} %bitcast.8), custom_call_target="tpu_custom_call" | custom-call | tf_op jit(solution)/shard_map/pallas_call | solution.py:486
  109.1 2.0 %copy.8 = f32[512,256]{1,0:T(8,128)} copy(f32[512,256]{0,1:T(8,128)} %bitcast.7) | data formatting | bytes 1048576

commit v3 on v2

--- a/solution.py
+++ b/solution.py
@@ -12,11 +12,12 @@
 NZ, NX, NY = 16, 4, 4
 
 
-def kernel(el_ref, scale_ref, hid_ref, u_ref, tgt_ref, gain_ref, o_ref, loss_ref,
-           hbuf, xbuf, tsrc, gain, in_sem, abuf, ubuf, acc, ssq, gbuf, tbuf, sta, stb, zst, lebuf, lbuf, pbuf, fin,
+def kernel(el_any, scale_any, hid_ref, u_ref, tgt_any, gain_any, o_ref, loss_ref,
+           el_ref, scale_ref, tgt_ref, gain_ref, hbuf, xbuf, tsrc, gain, in_sem,
+           abuf, ubuf, acc, accb, ssq, gbuf, tbuf, zst, zt, lebuf, tpair, lx, ly, pbuf, fin,
            r_o, r_d, r_c, q_o, q_d, q_c,
-           swap_sem, ring_s, ring_r, sib_s, sib_r, u_s, u_r, u_loc, t_sem, st_sem, z_s, z_r, le_sem,
-           g_sem, l_s, l_r, rs_s, rs_r, qs_s, qs_r):
+           swap_sem, ring_s, ring_r, sib_s, sib_r, u_s, u_r, u_loc, t_sem, lg_sem, z_s, z_r, zt_s, zt_r, le_sem,
+           tp_sem, l_s, l_r, rs_s, rs_r, qs_s, qs_r):
     dp = lax.axis_index("dp")
     vo = lax.axis_index("vocab")
     c = dp % 2
@@ -36,23 +37,17 @@
         return pltpu.make_async_remote_copy(src_ref=src, dst_ref=dst, send_sem=s, recv_sem=r,
                                             device_id=to, device_id_type=MESH)
 
-    hid_copy = pltpu.make_async_copy(hid_ref, hbuf, in_sem)
-    hid_copy.start()
-
     bar = pltpu.get_barrier_semaphore()
-
-    def hello(to):
+    for to in (sibling, partner, dev(x, y, (z + 1) % NZ, c), dev(x, y, (z + NZ - 1) % NZ, c)):
         pl.semaphore_signal(bar, inc=1, device_id=to, device_id_type=MESH)
-
-    hello(sibling)
-    hello(partner)
-
-    def hello_z(k, carry):
-        hello(dev(x, y, (z + k) % NZ, c))
-        hello(dev((x + k % 4) % 4, (y + k // 4) % 4, z, c))
-        return carry
-
-    lax.fori_loop(1, 16, hello_z, 0)
+    for k in range(1, 4):
+        pl.semaphore_signal(bar, inc=1, device_id=dev((x + k) % 4, y, z, c), device_id_type=MESH)
+        pl.semaphore_signal(bar, inc=1, device_id=dev(x, (y + k) % 4, z, c), device_id_type=MESH)
+
+    inputs = [pltpu.make_async_copy(a, b, in_sem.at[k]) for k, (a, b) in enumerate((
+        (hid_ref, hbuf), (el_any, el_ref), (scale_any, scale_ref), (tgt_any, tgt_ref), (gain_any, gain_ref)))]
+    for copy in inputs:
+        copy.start()
 
     def select(dst):
         for e in range(2):
@@ -60,7 +55,8 @@
                 dst[pl.ds(256 * e + 64 * row, 64), :] = hbuf[el_ref[e, row], pl.ds(64 * row, 64), :]
 
     mine = c == xh
-    hid_copy.wait()
+    for copy in inputs:
+        copy.wait()
 
     @pl.when(mine)
     def _():
@@ -70,7 +66,7 @@
     def _():
         select(xbuf)
 
-    pl.semaphore_wait(bar, 32)
+    pl.semaphore_wait(bar, 10)
 
     swap = rcopy(xbuf, abuf.at[1 - c, z], swap_sem.at[0], swap_sem.at[1], partner)
     swap_in = rcopy(xbuf, abuf.at[c, z], swap_sem.at[0], swap_sem.at[1], partner)
@@ -216,84 +212,113 @@
     r_row = lax.rsqrt(mean_sq + norm_eps)
     logits = acc[...] * r_row
     acc[...] = logits
+    lg_copy = rcopy(acc, accb, lg_sem.at[0], lg_sem.at[1], sibling)
+    lg_copy.start()
+
+    def as_tile(row):
+        return [row[:, 128 * k:128 * k + 128] for k in range(4)]
+
+    def as_row(tile):
+        return jnp.concatenate([tile[k:k + 1, :] for k in range(4)], axis=1)
+
+    m = jnp.max(logits, axis=0, keepdims=True)
+    ex = jnp.sum(jnp.exp(logits - m), axis=0, keepdims=True)
+    zst[z] = jnp.concatenate(as_tile(m) + as_tile(ex), axis=0)
+
+    def z_exchange(buf, ss, rr):
+        def out(k):
+            return rcopy(buf.at[z], buf.at[z], ss.at[k], rr.at[k], dev(x, y, (z + k) % NZ, c))
+
+        def into(k):
+            slot = (z + NZ - k) % NZ
+            return rcopy(buf.at[slot], buf.at[slot], ss.at[k], rr.at[k], dev(x, y, (z + k) % NZ, c))
+
+        def go(make, act):
+            def body(k, carry):
+                act(make(k))
+                return carry
+
+            lax.fori_loop(1, NZ, body, 0)
+
+        return (lambda: go(out, lambda a: a.start()), lambda: go(into, lambda a: a.wait_recv()),
+                lambda: go(out, lambda a: a.wait_send()))
+
+    z_start, z_wait, z_done = z_exchange(zst, z_s, z_r)
+    zt_start, zt_wait, zt_done = z_exchange(zt, zt_s, zt_r)
+    z_start()
+
     t_copy.wait_recv()
     t2x = jnp.where(mine, tsrc[0:2, :], tbuf[0:2, :])
     tgt = jnp.concatenate([t2x[0:1, :], t2x[1:2, :], t2x[0:1, :], t2x[1:2, :]], axis=1)
-    ids = (((c * NZ + z) * 256) + lax.broadcasted_iota(jnp.int32, (256, 512), 0)).astype(F32)
-    is_target = ids == tgt
-    m = jnp.max(logits, axis=0, keepdims=True)
-    sta[0:1, :] = m
-    sta[1:2, :] = jnp.sum(jnp.exp(logits - m), axis=0, keepdims=True)
-    sta[2:3, :] = jnp.sum(jnp.where(is_target, logits, 0.0), axis=0, keepdims=True)
-    st_copy = rcopy(sta, stb, st_sem.at[0], st_sem.at[1], sibling)
-    st_copy.start()
-    st_copy.wait_recv()
-    cols = pl.ds(pl.multiple_of(c * 256, 256), 256)
-    m_a, m_b = sta[0:1, cols], stb[0:1, cols]
-    m2 = jnp.maximum(m_a, m_b)
-    s2 = sta[1:2, cols] * jnp.exp(m_a - m2) + stb[1:2, cols] * jnp.exp(m_b - m2)
-    t2 = sta[2:3, cols] + stb[2:3, cols]
-    zst[z] = jnp.concatenate(
-        [m2[:, :128], m2[:, 128:], s2[:, :128], s2[:, 128:], t2[:, :128], t2[:, 128:], t2[:, :128], t2[:, 128:]], axis=0)
-
-    def z_copy(k):
-        return rcopy(zst.at[z], zst.at[z], z_s.at[k], z_r.at[k], dev(x, y, (z + k) % NZ, c))
-
-    def z_in(k):
-        slot = (z + NZ - k) % NZ
-        return rcopy(zst.at[slot], zst.at[slot], z_s.at[k], z_r.at[k], dev(x, y, (z + k) % NZ, c))
-
-    def z_start(k, carry):
-        z_copy(k).start()
-        return carry
-
-    def z_wait(k, carry):
-        z_in(k).wait_recv()
-        return carry
-
-    lax.fori_loop(1, NZ, z_start, 0)
-    lax.fori_loop(1, NZ, z_wait, 0)
+    scale_row = jnp.where(lax.broadcasted_iota(jnp.int32, (1, 512), 1) < 256, scale_ref[0], scale_ref[1])
+    rows_of = lax.broadcasted_iota(jnp.int32, (256, 512), 0)
+
+    def is_target(plane):
+        return (rows_of + (plane * NZ + z) * 256).astype(F32) == tgt
+
+    def lane_sum(row):
+        return row[:, :128] + row[:, 128:256] + row[:, 256:384] + row[:, 384:]
+
+    t_part = lane_sum(jnp.sum(jnp.where(is_target(c), logits, 0.0), axis=0, keepdims=True) * scale_row)
+    zt[z] = jnp.broadcast_to(t_part, (8, 128))
+
+    z_wait()
     st = zst[...]
-    m16, s16, t16 = st[:, 0:2, :], st[:, 2:4, :], st[:, 4:6, :]
+    m16, s16 = st[:, 0:4, :], st[:, 4:8, :]
     top = jnp.max(m16, axis=0)
-    lse = top + jnp.log(jnp.sum(s16 * jnp.exp(m16 - top[None]), axis=0))
-    t_all = jnp.sum(t16, axis=0)
-    lebuf[c] = jnp.concatenate([lse, t_all, lse, t_all], axis=0)
+    lebuf[c] = jnp.concatenate([top, jnp.sum(s16 * jnp.exp(m16 - top[None]), axis=0)], axis=0)
     le_copy = rcopy(lebuf.at[c], lebuf.at[c], le_sem.at[0], le_sem.at[1], sibling)
     le_in = rcopy(lebuf.at[1 - c], lebuf.at[1 - c], le_sem.at[0], le_sem.at[1], sibling)
     le_copy.start()
+    zt_start()
+    lg_copy.wait_recv()
     le_in.wait_recv()
-    lse_row = jnp.concatenate([lebuf[0, 0:1, :], lebuf[0, 1:2, :], lebuf[1, 0:1, :], lebuf[1, 1:2, :]], axis=1)
-    t_row = jnp.concatenate([lebuf[0, 2:3, :], lebuf[0, 3:4, :], lebuf[1, 2:3, :], lebuf[1, 3:4, :]], axis=1)
-    scale_row = jnp.where(lax.broadcasted_iota(jnp.int32, (1, 512), 1) < 256, scale_ref[0], scale_ref[1])
-    grad = (scale_row * r_row) * (jnp.exp(acc[...] - lse_row) - is_target.astype(F32))
-    gbuf[c] = grad.astype(BF16)
-    g_copy = rcopy(gbuf.at[c], gbuf.at[c], g_sem.at[0], g_sem.at[1], sibling)
-    g_in = rcopy(gbuf.at[1 - c], gbuf.at[1 - c], g_sem.at[0], g_sem.at[1], sibling)
-    g_copy.start()
-
-    loss4 = scale_row * (lse_row - t_row)
-    loss1 = loss4[:, :128] + loss4[:, 128:256] + loss4[:, 256:384] + loss4[:, 384:]
-    me = y * 4 + x
-    lbuf[me] = jnp.broadcast_to(loss1, (8, 128))
-
-    def l_copy(k):
-        return rcopy(lbuf.at[me], lbuf.at[me], l_s.at[k], l_r.at[k], dev((x + k % 4) % 4, (y + k // 4) % 4, z, c))
-
-    def l_in(k):
-        slot = (y + 4 - k // 4) % 4 * 4 + (x + 4 - k % 4) % 4
-        return rcopy(lbuf.at[slot], lbuf.at[slot], l_s.at[k], l_r.at[k], dev((x + k % 4) % 4, (y + k // 4) % 4, z, c))
-
-    def l_start(k, carry):
-        l_copy(k).start()
-        return carry
-
-    def l_wait(k, carry):
-        l_in(k).wait_recv()
-        l_copy(k).wait_send()
-        return carry
-
-    g_in.wait_recv()
+    m_a, m_b = lebuf[0, 0:4, :], lebuf[1, 0:4, :]
+    m_all = jnp.maximum(m_a, m_b)
+    lse = m_all + jnp.log(lebuf[0, 4:8, :] * jnp.exp(m_a - m_all) + lebuf[1, 4:8, :] * jnp.exp(m_b - m_all))
+    lse_row = as_row(lse)
+    weight = scale_row * r_row
+    gbuf[c] = (weight * (jnp.exp(acc[...] - lse_row) - is_target(c).astype(F32))).astype(BF16)
+    gbuf[1 - c] = (weight * (jnp.exp(accb[...] - lse_row) - is_target(1 - c).astype(F32))).astype(BF16)
+
+    def tp_exchange():
+        zt_wait()
+        tpair[c] = jnp.sum(zt[...], axis=0)
+        tp_copy.start()
+
+    tp_copy = rcopy(tpair.at[c], tpair.at[c], tp_sem.at[0], tp_sem.at[1], sibling)
+    tp_in = rcopy(tpair.at[1 - c], tpair.at[1 - c], tp_sem.at[0], tp_sem.at[1], sibling)
+
+    def l_copy(axis, k):
+        if axis == 0:
+            return rcopy(lx.at[x], lx.at[x], l_s.at[0, k], l_r.at[0, k], dev((x + k) % 4, y, z, c))
+        return rcopy(ly.at[y], ly.at[y], l_s.at[1, k], l_r.at[1, k], dev(x, (y + k) % 4, z, c))
+
+    def l_in(axis, k):
+        if axis == 0:
+            slot = (x + 4 - k) % 4
+            return rcopy(lx.at[slot], lx.at[slot], l_s.at[0, k], l_r.at[0, k], dev((x + k) % 4, y, z, c))
+        slot = (y + 4 - k) % 4
+        return rcopy(ly.at[slot], ly.at[slot], l_s.at[1, k], l_r.at[1, k], dev(x, (y + k) % 4, z, c))
+
+    def loss_x():
+        tp_in.wait_recv()
+        lx[x] = jnp.broadcast_to(lane_sum(scale_row * lse_row), (8, 128)) - (tpair[0] + tpair[1])
+        for k in range(1, 4):
+            l_copy(0, k).start()
+
+    def loss_y():
+        for k in range(1, 4):
+            l_in(0, k).wait_recv()
+        ly[y] = lx[0] + lx[1] + lx[2] + lx[3]
+        for k in range(1, 4):
+            l_copy(1, k).start()
+
+    def loss_end():
+        for k in range(1, 4):
+            l_in(1, k).wait_recv()
+        tot = ly[0] + ly[1] + ly[2] + ly[3]
+        loss_ref[0] = jnp.sum(tot[0:1, :]) * (1.0 / 4096.0)
 
     def along(axis, step):
         if axis == 0:
@@ -374,7 +399,7 @@
     start_d(0, 0)
     start_d(1, 0)
     grad_block(0, 0)
-    lax.fori_loop(1, 16, l_start, 0)
+    tp_exchange()
 
     for o in ORDER:
         for axis in range(2):
@@ -384,6 +409,7 @@
                 rows = part(axis, d)
                 ref[rows, :] = (ref[rows, :].astype(F32) + r_o[axis, d, o].astype(F32)).astype(BF16)
                 send_c(axis, d, o).start()
+    loss_x()
 
     for o in ORDER:
         for axis in range(2):
@@ -411,6 +437,7 @@
             ref[rows, :] = (ref[rows, :].astype(F32) + q_o[axis, d].astype(F32)).astype(BF16)
             send_c2(axis, d).start()
 
+    loss_y()
     s_own = ((y * 2 + xl) * 2 + c) * 2
     gain_own = jnp.concatenate([gain_row(s_own), gain_row(s_own + 1)], axis=1)
     for axis in range(2):
@@ -418,11 +445,10 @@
             send_c2(axis, w).wait_recv()
             send_d2(axis, 1 - w).wait_recv()
             rows = part(axis, w)
-            o_ref[rows, :] = (fin[rows, :] + q_c[axis, w].astype(F32) + q_d[axis, 1 - w].astype(F32)) * gain_own
-
-    lax.fori_loop(1, 16, l_wait, 0)
-    tot = jnp.sum(lbuf[...], axis=0)
-    loss_ref[0] = jnp.sum(tot[0:1, :]) * (1.0 / 4096.0)
+            fin[rows, :] = (fin[rows, :] + q_c[axis, w].astype(F32) + q_d[axis, 1 - w].astype(F32)) * gain_own
+        o_ref[:, 128 * axis:128 * axis + 128] = fin[pl.ds(128 * axis, 128), :].T
+
+    loss_end()
 
     for axis in range(2):
         for d in range(2):
@@ -433,14 +459,14 @@
             send_o2(axis, d).wait_send()
             send_d2(axis, d).wait_send()
             send_c2(axis, d).wait_send()
-    for copy in (t_copy, st_copy, le_copy, g_copy):
+    for axis in range(2):
+        for k in range(1, 4):
+            l_copy(axis, k).wait_send()
+    for copy in (t_copy, lg_copy, le_copy, tp_copy):
         copy.wait_send()
 
-    def z_done(k, carry):
-        z_copy(k).wait_send()
-        return carry
-
-    lax.fori_loop(1, NZ, z_done, 0)
+    z_done()
+    zt_done()
 
     def ring_done(i, carry):
         for h in range(2):
@@ -483,28 +509,32 @@
     smem = pl.BlockSpec(memory_space=pltpu.SMEM)
     anywhere = pl.BlockSpec(memory_space=pl.ANY)
     dma = pltpu.SemaphoreType.DMA
-    grad_t, loss = pl.pallas_call(
+    grad, loss = pl.pallas_call(
         kernel,
-        out_shape=(jax.ShapeDtypeStruct((256, 512), F32), jax.ShapeDtypeStruct((1,), F32)),
-        in_specs=[smem, smem, anywhere, anywhere, vmem, vmem],
+        out_shape=(jax.ShapeDtypeStruct((512, 256), F32), jax.ShapeDtypeStruct((1,), F32)),
+        in_specs=[anywhere] * 6,
         out_specs=(vmem, smem),
         scratch_shapes=[
+            pltpu.SMEM((2, 4), jnp.int32), pltpu.SMEM((2,), F32), pltpu.VMEM((2, 128), jnp.int32),
+            pltpu.VMEM((64, 128), BF16),
             pltpu.VMEM((4, 256, 256), BF16),
             pltpu.VMEM((512, 256), BF16),
             pltpu.VMEM((8, 128), F32),
             pltpu.VMEM((64, 128), F32),
-            dma,
+            dma((5,)),
             pltpu.VMEM((2, 16, 512, 256), BF16),
             pltpu.VMEM((32, 256, 256), BF16),
+            pltpu.VMEM((256, 512), F32),
             pltpu.VMEM((256, 512), F32),
             pltpu.VMEM((512, 128), F32),
             pltpu.VMEM((2, 256, 512), BF16),
             pltpu.VMEM((8, 128), F32),
-            pltpu.VMEM((8, 512), F32),
-            pltpu.VMEM((8, 512), F32),
+            pltpu.VMEM((16, 8, 128), F32),
             pltpu.VMEM((16, 8, 128), F32),
             pltpu.VMEM((2, 8, 128), F32),
-            pltpu.VMEM((16, 8, 128), F32),
+            pltpu.VMEM((2, 8, 128), F32),
+            pltpu.VMEM((4, 8, 128), F32),
+            pltpu.VMEM((4, 8, 128), F32),
             pltpu.VMEM((4, 4, 256, 512), BF16),
             pltpu.VMEM((256, 512), F32),
             pltpu.VMEM((2, 2, 4, 64, 512), BF16),
@@ -514,14 +544,14 @@
             pltpu.VMEM((2, 2, 64, 512), BF16),
             pltpu.VMEM((2, 2, 64, 512), BF16),
             dma((2,)), dma((2, 2, 8)), dma((2, 2, 8)), dma((16, 2)), dma((16, 2)),
-            dma((2, 8)), dma((2, 8)), dma, dma((2,)), dma((2,)), dma((16,)), dma((16,)), dma((2,)),
-            dma((2,)), dma((16,)), dma((16,)), dma((3, 2, 2, 4)), dma((3, 2, 2, 4)), dma((3, 2, 2)), dma((3, 2, 2)),
+            dma((2, 8)), dma((2, 8)), dma, dma((2,)), dma((2,)), dma((16,)), dma((16,)), dma((16,)), dma((16,)), dma((2,)),
+            dma((2,)), dma((2, 4)), dma((2, 4)), dma((3, 2, 2, 4)), dma((3, 2, 2, 4)), dma((3, 2, 2)), dma((3, 2, 2)),
         ],
         compiler_params=pltpu.CompilerParams(
             collective_id=0, has_side_effects=True, vmem_limit_bytes=56 << 20),
     )(exit_layers.T, exit_scale, hidden_states, unembedding.reshape(32, 256, 256),
       targets.reshape(2, 128), norm_gain.reshape(64, 128))
-    return (grad_t.T, loss.reshape(()))
+    return (grad, loss.reshape(()))
 
 
 def solution(mesh):

time: 115 us -> 111 us (0.965); the launches traced: 113 us -> 111 us
  Pallas kernels: 108 us -> 106 us
    pallas_call x1, Pallas kernels: 108 us -> 106 us  [per_device(): pl.pallas_call(kernel, out_shape=(jax.ShapeDtypeStruct((512, 256), F32),...]
where the time goes in v3:
time: 111 us
  Pallas kernels  106 us (95%)
  between operations  2.34 us (2%)
  local copies, waits for them, and re-layouts  1.87 us (2%)
    pallas_call x1, Pallas kernels, per_device(): pl.pallas_call(kernel, out_shape=(jax.ShapeDtypeStruct((512, 256), F32),...  106 us

profile of v3, /device:TPU:1, one launch (start us, length us, event | category | flops | bytes accessed | tf_op | source)
XLA Modules:
  0.0 110.7 jit_solution(14809870120315160834)
XLA Ops:
  0.6 106.5 %shard_map.77 = (f32[512,256]{1,0:T(8,128)}, f32[1]{0:T(128)}) custom-call(s32[2,4]{1,0:T(2,128)} %bitcast.7, f32[2]{0:T(128)} %scale_any.1, bf16[4,256,256]{2,1,0:T(8,128)(2,1)} %hid_ref.1, bf16[32,256,256]{2,1,0:T(8,128)(2,1)} %bitcast.5, s32[2,128]{1,0:T(2,128)} %bitcast.8, bf16[64,128]{1,0:T(8,128)(2,1)} %bitcast.6), custom_call_target="tpu_custom_call" | custom-call | tf_op jit(solution)/shard_map/pallas_call | solution.py:512
  107.1 1.9 %copy.10 = f32[512,256]{1,0:T(8,128)} copy(f32[512,256]{1,0:T(8,128)} %get-tuple-element.8) | data formatting | bytes 1048576

commit v4 on v3

--- a/solution.py
+++ b/solution.py
@@ -68,8 +68,13 @@
 
     pl.semaphore_wait(bar, 10)
 
-    swap = rcopy(xbuf, abuf.at[1 - c, z], swap_sem.at[0], swap_sem.at[1], partner)
-    swap_in = rcopy(xbuf, abuf.at[c, z], swap_sem.at[0], swap_sem.at[1], partner)
+    def swap(h):
+        rows = pl.ds(256 * h, 256)
+        return rcopy(xbuf.at[rows], abuf.at[1 - c, z, rows], swap_sem.at[0, h], swap_sem.at[1, h], partner)
+
+    def swap_in(h):
+        ref = abuf.at[c, z, pl.ds(256 * h, 256)]
+        return rcopy(ref, ref, swap_sem.at[0, h], swap_sem.at[1, h], partner)
 
     def u_direct(k):
         j = (1 - xl) * 8 + k
@@ -91,7 +96,8 @@
 
     @pl.when(jnp.logical_not(mine))
     def _():
-        swap.start()
+        for h in range(2):
+            swap(h).start()
 
     tsrc[0:2, :] = tgt_ref[...].astype(F32)
     t_copy = rcopy(tsrc, tbuf, t_sem.at[0], t_sem.at[1], sibling)
@@ -106,10 +112,6 @@
             return carry
 
         lax.fori_loop(0, 8, send_u, 0)
-
-    @pl.when(jnp.logical_not(mine))
-    def _():
-        swap_in.wait_recv()
 
     def step_slot(d, i):
         return (z - i + NZ) % NZ if d == 0 else (z + i) % NZ
@@ -136,6 +138,10 @@
         return rcopy(ref, ref, sib_s.at[n, h], sib_r.at[n, h], sibling)
 
     for h in range(2):
+        @pl.when(jnp.logical_not(mine))
+        def _():
+            swap_in(h).wait_recv()
+
         for d in range(2):
             ring(d, h, 1).start()
     for h in range(2):
@@ -146,7 +152,7 @@
     def gain_row(s):
         return jnp.concatenate([gain[pl.ds(2 * s, 1), :], gain[pl.ds(2 * s + 1, 1), :]], axis=1)
 
-    acc[...] = jnp.zeros_like(acc)
+    acc[0:256, :] = jnp.zeros((256, 512), F32)
     ssq[...] = jnp.zeros_like(ssq)
 
     def ring_step(i, more):
@@ -170,7 +176,7 @@
             a = abuf[cs, slot].astype(F32)
             ssq[...] += a[:, :128] * a[:, :128] + a[:, 128:] * a[:, 128:]
             ag = (a * gain_row(s)).astype(BF16)
-            acc[...] += lax.dot_general(ubuf[s], ag, (((0,), (1,)), ((), ())), preferred_element_type=F32)
+            acc[0:256, :] += lax.dot_general(ubuf[s], ag, (((0,), (1,)), ((), ())), preferred_element_type=F32)
         return carry
 
     def loop_step(i, carry):
@@ -202,19 +208,15 @@
     ring_step(6, 2)
     lax.fori_loop(5, 10, blocks, 0)
     ring_step(7, 1)
-    lax.fori_loop(10, 13, blocks, 0)
+    lax.fori_loop(10, 15, blocks, 0)
     for d in range(2):
         ring_in(d, d, 8).wait_recv()
         sib(15, (z + 8) % NZ, d).start()
-    lax.fori_loop(13, 16, blocks, 0)
+    blocks(15, 0)
 
     mean_sq = jnp.sum(ssq[...].T, axis=0, keepdims=True) * (1.0 / 8192.0)
     r_row = lax.rsqrt(mean_sq + norm_eps)
-    logits = acc[...] * r_row
-    acc[...] = logits
-    lg_copy = rcopy(acc, accb, lg_sem.at[0], lg_sem.at[1], sibling)
-    lg_copy.start()
-
+    logits = acc[0:256, :] * r_row
     def as_tile(row):
         return [row[:, 128 * k:128 * k + 128] for k in range(4)]
 
@@ -222,8 +224,10 @@
         return jnp.concatenate([tile[k:k + 1, :] for k in range(4)], axis=1)
 
     m = jnp.max(logits, axis=0, keepdims=True)
-    ex = jnp.sum(jnp.exp(logits - m), axis=0, keepdims=True)
-    zst[z] = jnp.concatenate(as_tile(m) + as_tile(ex), axis=0)
+    ex = jnp.exp(logits - m)
+    acc[0:256, :] = ex
+    acc[256:264, :] = jnp.broadcast_to(m, (8, 512))
+    zst[z] = jnp.concatenate(as_tile(m) + as_tile(jnp.sum(ex, axis=0, keepdims=True)), axis=0)
 
     def z_exchange(buf, ss, rr):
         def out(k):
@@ -246,6 +250,8 @@
     z_start, z_wait, z_done = z_exchange(zst, z_s, z_r)
     zt_start, zt_wait, zt_done = z_exchange(zt, zt_s, zt_r)
     z_start()
+    lg_copy = rcopy(acc, accb, lg_sem.at[0], lg_sem.at[1], sibling)
+    lg_copy.start()
 
     t_copy.wait_recv()
     t2x = jnp.where(mine, tsrc[0:2, :], tbuf[0:2, :])
@@ -270,7 +276,6 @@
     le_copy = rcopy(lebuf.at[c], lebuf.at[c], le_sem.at[0], le_sem.at[1], sibling)
     le_in = rcopy(lebuf.at[1 - c], lebuf.at[1 - c], le_sem.at[0], le_sem.at[1], sibling)
     le_copy.start()
-    zt_start()
     lg_copy.wait_recv()
     le_in.wait_recv()
     m_a, m_b = lebuf[0, 0:4, :], lebuf[1, 0:4, :]
@@ -278,8 +283,13 @@
     lse = m_all + jnp.log(lebuf[0, 4:8, :] * jnp.exp(m_a - m_all) + lebuf[1, 4:8, :] * jnp.exp(m_b - m_all))
     lse_row = as_row(lse)
     weight = scale_row * r_row
-    gbuf[c] = (weight * (jnp.exp(acc[...] - lse_row) - is_target(c).astype(F32))).astype(BF16)
-    gbuf[1 - c] = (weight * (jnp.exp(accb[...] - lse_row) - is_target(1 - c).astype(F32))).astype(BF16)
+
+    def gradient(plane, buf):
+        share = jnp.exp(buf[256:257, :] - lse_row)
+        gbuf[plane] = (weight * (buf[0:256, :] * share - is_target(plane).astype(F32))).astype(BF16)
+
+    gradient(c, acc)
+    gradient(1 - c, accb)
 
     def tp_exchange():
         zt_wait()
@@ -369,49 +379,19 @@
         for d in range(2):
             send_d(axis, d, o).start()
 
-    ORDER = (2, 1, 3, 0)
-    grad_block(2, 2)
-    start_o(0, 2)
-    start_o(1, 2)
-
-    def o_blocks(k, carry):
-        o = k
-        grad_block(o, 2)
-        start_o(0, o)
-        grad_block(2, o)
-        start_o(1, o)
-        return carry
-
-    o_blocks(1, 0)
-    o_blocks(3, 0)
-    o_blocks(0, 0)
-    start_d(0, 2)
-    start_d(1, 2)
-    for dy in (1, 3):
-        for dx in (1, 3):
-            grad_block(dy, dx)
-    for o in (1, 3):
-        start_d(0, o)
-        start_d(1, o)
-    for dd in (1, 3):
-        grad_block(0, dd)
-        grad_block(dd, 0)
-    start_d(0, 0)
-    start_d(1, 0)
-    grad_block(0, 0)
-    tp_exchange()
-
-    for o in ORDER:
+    def pair_sum(axis, d, o):
+        send_o(axis, d, o).wait_recv()
+        ref = blk(axis, STEP[d], o)
+        rows = part(axis, d)
+        ref[rows, :] = ref[rows, :] + r_o[axis, d, o]
+        send_c(axis, d, o).start()
+
+    def pair_sums(o):
         for axis in range(2):
             for d in range(2):
-                send_o(axis, d, o).wait_recv()
-                ref = blk(axis, STEP[d], o)
-                rows = part(axis, d)
-                ref[rows, :] = (ref[rows, :].astype(F32) + r_o[axis, d, o].astype(F32)).astype(BF16)
-                send_c(axis, d, o).start()
-    loss_x()
-
-    for o in ORDER:
+                pair_sum(axis, d, o)
+
+    def first_pass(o):
         for axis in range(2):
             own = blk(axis, 0, o)
             for w in range(2):
@@ -423,21 +403,52 @@
                     fin[rows, :] = total
                 else:
                     own[rows, :] = total.astype(BF16)
-            if o == 2:
-                for d in range(2):
-                    send_o2(axis, d).start()
+                if o == 2:
+                    send_o2(axis, w).start()
             if o in STEP:
                 send_d2(axis, STEP.index(o)).start()
 
+    def both(start, o):
+        for axis in range(2):
+            start(axis, o)
+
+    grad_block(2, 2)
+    both(start_o, 2)
+    for o in (1, 3, 0):
+        grad_block(o, 2)
+        start_o(0, o)
+        grad_block(2, o)
+        start_o(1, o)
+    both(start_d, 2)
+    zt_start()
+    pair_sums(2)
+    for dy in (1, 3):
+        for dx in (1, 3):
+            grad_block(dy, dx)
+    both(start_d, 1)
+    both(start_d, 3)
+    pair_sums(1)
+    pair_sums(3)
+    tp_exchange()
+    first_pass(2)
+    for k in (1, 3):
+        grad_block(0, k)
+        grad_block(k, 0)
+    both(start_d, 0)
+    pair_sums(0)
+    loss_x()
+    first_pass(1)
+    first_pass(3)
+    loss_y()
+    grad_block(0, 0)
     for axis in range(2):
         for d in range(2):
             send_o2(axis, d).wait_recv()
             ref = blk(axis, 0, STEP[d])
             rows = part(axis, d)
-            ref[rows, :] = (ref[rows, :].astype(F32) + q_o[axis, d].astype(F32)).astype(BF16)
+            ref[rows, :] = ref[rows, :] + q_o[axis, d]
             send_c2(axis, d).start()
-
-    loss_y()
+    first_pass(0)
     s_own = ((y * 2 + xl) * 2 + c) * 2
     gain_own = jnp.concatenate([gain_row(s_own), gain_row(s_own + 1)], axis=1)
     for axis in range(2):
@@ -495,7 +506,8 @@
 
     @pl.when(jnp.logical_not(mine))
     def _():
-        swap.wait_send()
+        for h in range(2):
+            swap(h).wait_send()
 
         def done(k, carry):
             u_mate(k).wait_send()
@@ -507,7 +519,7 @@
 def per_device(hidden_states, exit_layers, targets, norm_gain, exit_scale, unembedding):
     vmem = pl.BlockSpec(memory_space=pltpu.VMEM)
     smem = pl.BlockSpec(memory_space=pltpu.SMEM)
-    anywhere = pl.BlockSpec(memory_space=pl.ANY)
+    anywhere = pl.BlockSpec(memory_space=pltpu.HBM)
     dma = pltpu.SemaphoreType.DMA
     grad, loss = pl.pallas_call(
         kernel,
@@ -524,8 +536,8 @@
             dma((5,)),
             pltpu.VMEM((2, 16, 512, 256), BF16),
             pltpu.VMEM((32, 256, 256), BF16),
-            pltpu.VMEM((256, 512), F32),
-            pltpu.VMEM((256, 512), F32),
+            pltpu.VMEM((264, 512), F32),
+            pltpu.VMEM((264, 512), F32),
             pltpu.VMEM((512, 128), F32),
             pltpu.VMEM((2, 256, 512), BF16),
             pltpu.VMEM((8, 128), F32),
@@ -543,14 +555,15 @@
             pltpu.VMEM((2, 2, 64, 512), BF16),
             pltpu.VMEM((2, 2, 64, 512), BF16),
             pltpu.VMEM((2, 2, 64, 512), BF16),
-            dma((2,)), dma((2, 2, 8)), dma((2, 2, 8)), dma((16, 2)), dma((16, 2)),
+            dma((2, 2)), dma((2, 2, 8)), dma((2, 2, 8)), dma((16, 2)), dma((16, 2)),
             dma((2, 8)), dma((2, 8)), dma, dma((2,)), dma((2,)), dma((16,)), dma((16,)), dma((16,)), dma((16,)), dma((2,)),
             dma((2,)), dma((2, 4)), dma((2, 4)), dma((3, 2, 2, 4)), dma((3, 2, 2, 4)), dma((3, 2, 2)), dma((3, 2, 2)),
         ],
         compiler_params=pltpu.CompilerParams(
-            collective_id=0, has_side_effects=True, vmem_limit_bytes=56 << 20),
-    )(exit_layers.T, exit_scale, hidden_states, unembedding.reshape(32, 256, 256),
-      targets.reshape(2, 128), norm_gain.reshape(64, 128))
+            collective_id=0, has_side_effects=True, vmem_limit_bytes=30 << 20),
+    )(*[pltpu.with_memory_space_constraint(a, pltpu.HBM) for a in (
+        exit_layers.T, exit_scale, hidden_states, unembedding.reshape(32, 256, 256),
+        targets.reshape(2, 128), norm_gain.reshape(64, 128))])
     return (grad, loss.reshape(()))
 
 

time: 111 us -> 107 us (0.964)
  Pallas kernels: 106 us -> 104 us
    pallas_call x1, Pallas kernels: 106 us -> 104 us  [per_device(): pl.pallas_call(kernel, out_shape=(jax.ShapeDtypeStruct((512, 256), F32),...]
where the time goes in v4:
time: 107 us
  Pallas kernels  104 us (97%)
  between operations  2.33 us (2%)
    pallas_call x1, Pallas kernels, per_device(): pl.pallas_call(kernel, out_shape=(jax.ShapeDtypeStruct((512, 256), F32),...  104 us

profile of v4, /device:TPU:1, one launch (start us, length us, event | category | flops | bytes accessed | tf_op | source)
XLA Modules:
  0.0 107.0 jit_solution(3172389574412631123)
XLA Ops:
  0.6 103.8 %shard_map.77 = (f32[512,256]{1,0:T(8,128)S(1)}, f32[1]{0:T(128)}) custom-call(s32[2,4]{1,0:T(2,128)} %bitcast.7, f32[2]{0:T(128)} %scale_any.1, bf16[4,256,256]{2,1,0:T(8,128)(2,1)} %hid_ref.1, bf16[32,256,256]{2,1,0:T(8,128)(2,1)} %bitcast.5, s32[2,128]{1,0:T(2,128)} %bitcast.8, bf16[64,128]{1,0:T(8,128)(2,1)} %bitcast.6), custom_call_target="tpu_custom_call" | custom-call | tf_op jit(solution)/shard_map/pallas_call | solution.py:524
  104.5 0.8 copy.10

commit v5 on v4

--- a/solution.py
+++ b/solution.py
@@ -14,10 +14,10 @@
 
 def kernel(el_any, scale_any, hid_ref, u_ref, tgt_any, gain_any, o_ref, loss_ref,
            el_ref, scale_ref, tgt_ref, gain_ref, hbuf, xbuf, tsrc, gain, in_sem,
-           abuf, ubuf, acc, accb, ssq, gbuf, tbuf, zst, zt, lebuf, tpair, lx, ly, pbuf, fin,
+           abuf, ubuf, acc, accb, ssq, gbuf, tbuf, zst, lebuf, lx, ly, pbuf, fin,
            r_o, r_d, r_c, q_o, q_d, q_c,
-           swap_sem, ring_s, ring_r, sib_s, sib_r, u_s, u_r, u_loc, t_sem, lg_sem, z_s, z_r, zt_s, zt_r, le_sem,
-           tp_sem, l_s, l_r, rs_s, rs_r, qs_s, qs_r):
+           swap_sem, ring_s, ring_r, sib_s, sib_r, u_s, u_r, u_loc, t_sem, lg_sem, z_s, z_r, le_sem,
+           l_s, l_r, rs_s, rs_r, qs_s, qs_r):
     dp = lax.axis_index("dp")
     vo = lax.axis_index("vocab")
     c = dp % 2
@@ -214,75 +214,65 @@
         sib(15, (z + 8) % NZ, d).start()
     blocks(15, 0)
 
+    t_copy.wait_recv()
+    t2x = jnp.where(mine, tsrc[0:2, :], tbuf[0:2, :])
+    tgt = jnp.concatenate([t2x[0:1, :], t2x[1:2, :], t2x[0:1, :], t2x[1:2, :]], axis=1)
+    scale_row = jnp.where(lax.broadcasted_iota(jnp.int32, (1, 512), 1) < 256, scale_ref[0], scale_ref[1])
     mean_sq = jnp.sum(ssq[...].T, axis=0, keepdims=True) * (1.0 / 8192.0)
     r_row = lax.rsqrt(mean_sq + norm_eps)
-    logits = acc[0:256, :] * r_row
+
     def as_tile(row):
         return [row[:, 128 * k:128 * k + 128] for k in range(4)]
 
-    def as_row(tile):
-        return jnp.concatenate([tile[k:k + 1, :] for k in range(4)], axis=1)
-
+    def lane_sum(row):
+        return row[:, :128] + row[:, 128:256] + row[:, 256:384] + row[:, 384:]
+
+    def is_target(plane):
+        return lax.broadcasted_iota(jnp.int32, (256, 512), 0).astype(F32) == tgt - ((plane * NZ + z) * 256).astype(F32)
+
+    logits = acc[0:256, :] * r_row
     m = jnp.max(logits, axis=0, keepdims=True)
     ex = jnp.exp(logits - m)
     acc[0:256, :] = ex
     acc[256:264, :] = jnp.broadcast_to(m, (8, 512))
-    zst[z] = jnp.concatenate(as_tile(m) + as_tile(jnp.sum(ex, axis=0, keepdims=True)), axis=0)
-
-    def z_exchange(buf, ss, rr):
-        def out(k):
-            return rcopy(buf.at[z], buf.at[z], ss.at[k], rr.at[k], dev(x, y, (z + k) % NZ, c))
-
-        def into(k):
-            slot = (z + NZ - k) % NZ
-            return rcopy(buf.at[slot], buf.at[slot], ss.at[k], rr.at[k], dev(x, y, (z + k) % NZ, c))
-
-        def go(make, act):
-            def body(k, carry):
-                act(make(k))
-                return carry
-
-            lax.fori_loop(1, NZ, body, 0)
-
-        return (lambda: go(out, lambda a: a.start()), lambda: go(into, lambda a: a.wait_recv()),
-                lambda: go(out, lambda a: a.wait_send()))
-
-    z_start, z_wait, z_done = z_exchange(zst, z_s, z_r)
-    zt_start, zt_wait, zt_done = z_exchange(zt, zt_s, zt_r)
-    z_start()
+    part_lse = m + jnp.log(jnp.sum(ex, axis=0, keepdims=True))
+    part_t = lane_sum(jnp.sum(jnp.where(is_target(c), logits, 0.0), axis=0, keepdims=True) * scale_row)
+    zst[z] = jnp.concatenate(as_tile(part_lse) + [part_t] * 4, axis=0)
+
+    def z_copy(k):
+        return rcopy(zst.at[z], zst.at[z], z_s.at[k], z_r.at[k], dev(x, y, (z + k) % NZ, c))
+
+    def z_in(k):
+        slot = (z + NZ - k) % NZ
+        return rcopy(zst.at[slot], zst.at[slot], z_s.at[k], z_r.at[k], dev(x, y, (z + k) % NZ, c))
+
+    def z_all(act):
+        def body(k, carry):
+            act(k)
+            return carry
+
+        lax.fori_loop(1, NZ, body, 0)
+
+    z_all(lambda k: z_copy(k).start())
     lg_copy = rcopy(acc, accb, lg_sem.at[0], lg_sem.at[1], sibling)
     lg_copy.start()
-
-    t_copy.wait_recv()
-    t2x = jnp.where(mine, tsrc[0:2, :], tbuf[0:2, :])
-    tgt = jnp.concatenate([t2x[0:1, :], t2x[1:2, :], t2x[0:1, :], t2x[1:2, :]], axis=1)
-    scale_row = jnp.where(lax.broadcasted_iota(jnp.int32, (1, 512), 1) < 256, scale_ref[0], scale_ref[1])
-    rows_of = lax.broadcasted_iota(jnp.int32, (256, 512), 0)
-
-    def is_target(plane):
-        return (rows_of + (plane * NZ + z) * 256).astype(F32) == tgt
-
-    def lane_sum(row):
-        return row[:, :128] + row[:, 128:256] + row[:, 256:384] + row[:, 384:]
-
-    t_part = lane_sum(jnp.sum(jnp.where(is_target(c), logits, 0.0), axis=0, keepdims=True) * scale_row)
-    zt[z] = jnp.broadcast_to(t_part, (8, 128))
-
-    z_wait()
+    weight = scale_row * r_row
+    z_all(lambda k: z_in(k).wait_recv())
+
     st = zst[...]
-    m16, s16 = st[:, 0:4, :], st[:, 4:8, :]
-    top = jnp.max(m16, axis=0)
-    lebuf[c] = jnp.concatenate([top, jnp.sum(s16 * jnp.exp(m16 - top[None]), axis=0)], axis=0)
+    l16 = st[:, 0:4, :]
+    top = jnp.max(l16, axis=0)
+    plane_lse = top + jnp.log(jnp.sum(jnp.exp(l16 - top[None]), axis=0))
+    lebuf[c] = jnp.concatenate([plane_lse, jnp.sum(st[:, 4:8, :], axis=0)], axis=0)
     le_copy = rcopy(lebuf.at[c], lebuf.at[c], le_sem.at[0], le_sem.at[1], sibling)
     le_in = rcopy(lebuf.at[1 - c], lebuf.at[1 - c], le_sem.at[0], le_sem.at[1], sibling)
     le_copy.start()
     lg_copy.wait_recv()
     le_in.wait_recv()
-    m_a, m_b = lebuf[0, 0:4, :], lebuf[1, 0:4, :]
-    m_all = jnp.maximum(m_a, m_b)
-    lse = m_all + jnp.log(lebuf[0, 4:8, :] * jnp.exp(m_a - m_all) + lebuf[1, 4:8, :] * jnp.exp(m_b - m_all))
-    lse_row = as_row(lse)
-    weight = scale_row * r_row
+    l_a, l_b = lebuf[0, 0:4, :], lebuf[1, 0:4, :]
+    l_top = jnp.maximum(l_a, l_b)
+    lse = l_top + jnp.log(jnp.exp(l_a - l_top) + jnp.exp(l_b - l_top))
+    lse_row = jnp.concatenate([lse[k:k + 1, :] for k in range(4)], axis=1)
 
     def gradient(plane, buf):
         share = jnp.exp(buf[256:257, :] - lse_row)
@@ -290,14 +280,6 @@
 
     gradient(c, acc)
     gradient(1 - c, accb)
-
-    def tp_exchange():
-        zt_wait()
-        tpair[c] = jnp.sum(zt[...], axis=0)
-        tp_copy.start()
-
-    tp_copy = rcopy(tpair.at[c], tpair.at[c], tp_sem.at[0], tp_sem.at[1], sibling)
-    tp_in = rcopy(tpair.at[1 - c], tpair.at[1 - c], tp_sem.at[0], tp_sem.at[1], sibling)
 
     def l_copy(axis, k):
         if axis == 0:
@@ -312,8 +294,8 @@
         return rcopy(ly.at[slot], ly.at[slot], l_s.at[1, k], l_r.at[1, k], dev(x, (y + k) % 4, z, c))
 
     def loss_x():
-        tp_in.wait_recv()
-        lx[x] = jnp.broadcast_to(lane_sum(scale_row * lse_row), (8, 128)) - (tpair[0] + tpair[1])
+        lx[x] = jnp.broadcast_to(lane_sum(scale_row * lse_row), (8, 128)) - (
+            jnp.broadcast_to(lebuf[0, 4:5, :], (8, 128)) + jnp.broadcast_to(lebuf[1, 4:5, :], (8, 128)))
         for k in range(1, 4):
             l_copy(0, k).start()
 
@@ -420,7 +402,7 @@
         grad_block(2, o)
         start_o(1, o)
     both(start_d, 2)
-    zt_start()
+    loss_x()
     pair_sums(2)
     for dy in (1, 3):
         for dx in (1, 3):
@@ -429,17 +411,15 @@
     both(start_d, 3)
     pair_sums(1)
     pair_sums(3)
-    tp_exchange()
     first_pass(2)
     for k in (1, 3):
         grad_block(0, k)
         grad_block(k, 0)
     both(start_d, 0)
     pair_sums(0)
-    loss_x()
+    loss_y()
     first_pass(1)
     first_pass(3)
-    loss_y()
     grad_block(0, 0)
     for axis in range(2):
         for d in range(2):
@@ -473,11 +453,10 @@
     for axis in range(2):
         for k in range(1, 4):
             l_copy(axis, k).wait_send()
-    for copy in (t_copy, lg_copy, le_copy, tp_copy):
+    for copy in (t_copy, lg_copy, le_copy):
         copy.wait_send()
 
-    z_done()
-    zt_done()
+    z_all(lambda k: z_copy(k).wait_send())
 
     def ring_done(i, carry):
         for h in range(2):
@@ -542,8 +521,6 @@
             pltpu.VMEM((2, 256, 512), BF16),
             pltpu.VMEM((8, 128), F32),
             pltpu.VMEM((16, 8, 128), F32),
-            pltpu.VMEM((16, 8, 128), F32),
-            pltpu.VMEM((2, 8, 128), F32),
             pltpu.VMEM((2, 8, 128), F32),
             pltpu.VMEM((4, 8, 128), F32),
             pltpu.VMEM((4, 8, 128), F32),
@@ -556,8 +533,8 @@
             pltpu.VMEM((2, 2, 64, 512), BF16),
             pltpu.VMEM((2, 2, 64, 512), BF16),
             dma((2, 2)), dma((2, 2, 8)), dma((2, 2, 8)), dma((16, 2)), dma((16, 2)),
-            dma((2, 8)), dma((2, 8)), dma, dma((2,)), dma((2,)), dma((16,)), dma((16,)), dma((16,)), dma((16,)), dma((2,)),
-            dma((2,)), dma((2, 4)), dma((2, 4)), dma((3, 2, 2, 4)), dma((3, 2, 2, 4)), dma((3, 2, 2)), dma((3, 2, 2)),
+            dma((2, 8)), dma((2, 8)), dma, dma((2,)), dma((2,)), dma((16,)), dma((16,)), dma((2,)),
+            dma((2, 4)), dma((2, 4)), dma((3, 2, 2, 4)), dma((3, 2, 2, 4)), dma((3, 2, 2)), dma((3, 2, 2)),
         ],
         compiler_params=pltpu.CompilerParams(
             collective_id=0, has_side_effects=True, vmem_limit_bytes=30 << 20),

time: 107 us -> 105 us (0.981)
  Pallas kernels: 104 us -> 101 us
    pallas_call x1, Pallas kernels: 104 us -> 101 us  [per_device(): pl.pallas_call(kernel, out_shape=(jax.ShapeDtypeStruct((512, 256), F32),...]
where the time goes in v5:
time: 105 us; the launch traced here: 104 us
  Pallas kernels  101 us (96%)
  between operations  2.33 us (2%)
    pallas_call x1, Pallas kernels, per_device(): pl.pallas_call(kernel, out_shape=(jax.ShapeDtypeStruct((512, 256), F32),...  101 us

profile of v5, /device:TPU:1, one launch (start us, length us, event | category | flops | bytes accessed | tf_op | source)
XLA Modules:
  0.0 104.4 jit_solution(16528101361994480550)
XLA Ops:
  0.6 101.2 %shard_map.77 = (f32[512,256]{1,0:T(8,128)S(1)}, f32[1]{0:T(128)}) custom-call(s32[2,4]{1,0:T(2,128)} %bitcast.7, f32[2]{0:T(128)} %scale_any.1, bf16[4,256,256]{2,1,0:T(8,128)(2,1)} %hid_ref.1, bf16[32,256,256]{2,1,0:T(8,128)(2,1)} %bitcast.5, s32[2,128]{1,0:T(2,128)} %bitcast.8, bf16[64,128]{1,0:T(8,128)(2,1)} %bitcast.6), custom_call_target="tpu_custom_call" | custom-call | tf_op jit(solution)/shard_map/pallas_call | solution.py:503
  101.9 0.8 copy.10

commit v6 on v5

--- a/solution.py
+++ b/solution.py
@@ -14,7 +14,7 @@
 
 def kernel(el_any, scale_any, hid_ref, u_ref, tgt_any, gain_any, o_ref, loss_ref,
            el_ref, scale_ref, tgt_ref, gain_ref, hbuf, xbuf, tsrc, gain, in_sem,
-           abuf, ubuf, acc, accb, ssq, gbuf, tbuf, zst, lebuf, lx, ly, pbuf, fin,
+           abuf, ubuf, acc, ssq, gbuf, tbuf, zst, lebuf, lx, ly, pbuf, fin,
            r_o, r_d, r_c, q_o, q_d, q_c,
            swap_sem, ring_s, ring_r, sib_s, sib_r, u_s, u_r, u_loc, t_sem, lg_sem, z_s, z_r, le_sem,
            l_s, l_r, rs_s, rs_r, qs_s, qs_r):
@@ -37,6 +37,11 @@
         return pltpu.make_async_remote_copy(src_ref=src, dst_ref=dst, send_sem=s, recv_sem=r,
                                             device_id=to, device_id_type=MESH)
 
+    inputs = [pltpu.make_async_copy(a, b, in_sem.at[k]) for k, (a, b) in enumerate((
+        (hid_ref, hbuf), (el_any, el_ref), (scale_any, scale_ref), (tgt_any, tgt_ref), (gain_any, gain_ref)))]
+    for copy in inputs[:2]:
+        copy.start()
+
     bar = pltpu.get_barrier_semaphore()
     for to in (sibling, partner, dev(x, y, (z + 1) % NZ, c), dev(x, y, (z + NZ - 1) % NZ, c)):
         pl.semaphore_signal(bar, inc=1, device_id=to, device_id_type=MESH)
@@ -44,9 +49,7 @@
         pl.semaphore_signal(bar, inc=1, device_id=dev((x + k) % 4, y, z, c), device_id_type=MESH)
         pl.semaphore_signal(bar, inc=1, device_id=dev(x, (y + k) % 4, z, c), device_id_type=MESH)
 
-    inputs = [pltpu.make_async_copy(a, b, in_sem.at[k]) for k, (a, b) in enumerate((
-        (hid_ref, hbuf), (el_any, el_ref), (scale_any, scale_ref), (tgt_any, tgt_ref), (gain_any, gain_ref)))]
-    for copy in inputs:
+    for copy in inputs[2:]:
         copy.start()
 
     def select(dst):
@@ -55,7 +58,7 @@
                 dst[pl.ds(256 * e + 64 * row, 64), :] = hbuf[el_ref[e, row], pl.ds(64 * row, 64), :]
 
     mine = c == xh
-    for copy in inputs:
+    for copy in inputs[:2]:
         copy.wait()
 
     @pl.when(mine)
@@ -99,20 +102,6 @@
         for h in range(2):
             swap(h).start()
 
-    tsrc[0:2, :] = tgt_ref[...].astype(F32)
-    t_copy = rcopy(tsrc, tbuf, t_sem.at[0], t_sem.at[1], sibling)
-    t_copy.start()
-
-    @pl.when(mine)
-    def _():
-        u_local.start()
-
-        def send_u(k, carry):
-            u_direct(k).start()
-            return carry
-
-        lax.fori_loop(0, 8, send_u, 0)
-
     def step_slot(d, i):
         return (z - i + NZ) % NZ if d == 0 else (z + i) % NZ
 
@@ -129,13 +118,13 @@
         to = dev(x, y, (z + 1) % NZ, c) if d == 0 else dev(x, y, (z + NZ - 1) % NZ, c)
         return rcopy(ref, ref, ring_s.at[d, h, i - 1], ring_r.at[d, h, i - 1], to)
 
-    def sib(n, slot, h):
-        ref = half(slot, h)
-        return rcopy(ref, ref, sib_s.at[n, h], sib_r.at[n, h], sibling)
-
-    def sib_in(n, slot, h):
-        ref = abuf.at[1 - c, slot, pl.ds(256 * h, 256)]
-        return rcopy(ref, ref, sib_s.at[n, h], sib_r.at[n, h], sibling)
+    def sib(n, slot):
+        ref = abuf.at[c, slot]
+        return rcopy(ref, ref, sib_s.at[n], sib_r.at[n], sibling)
+
+    def sib_in(n, slot):
+        ref = abuf.at[1 - c, slot]
+        return rcopy(ref, ref, sib_s.at[n], sib_r.at[n], sibling)
 
     for h in range(2):
         @pl.when(jnp.logical_not(mine))
@@ -144,15 +133,30 @@
 
         for d in range(2):
             ring(d, h, 1).start()
-    for h in range(2):
-        sib(0, z, h).start()
+    sib(0, z).start()
+
+    for copy in inputs[2:]:
+        copy.wait()
+    tsrc[0:2, :] = tgt_ref[...].astype(F32)
+    t_copy = rcopy(tsrc, tbuf, t_sem.at[0], t_sem.at[1], sibling)
+    t_copy.start()
+
+    @pl.when(mine)
+    def _():
+        def send_u(k, carry):
+            u_direct(k).start()
+            return carry
+
+        lax.fori_loop(0, 8, send_u, 0)
+        u_local.start()
+
 
     gain[...] = gain_ref[...].astype(F32)
 
     def gain_row(s):
         return jnp.concatenate([gain[pl.ds(2 * s, 1), :], gain[pl.ds(2 * s + 1, 1), :]], axis=1)
 
-    acc[0:256, :] = jnp.zeros((256, 512), F32)
+    acc[c, 0:256, :] = jnp.zeros((256, 512), F32)
     ssq[...] = jnp.zeros_like(ssq)
 
     def ring_step(i, more):
@@ -161,7 +165,8 @@
                 ring_in(d, h, i).wait_recv()
                 if more == 2 or (more == 1 and h == d):
                     ring(d, h, i + 1).start()
-                sib(2 * i - d, step_slot(d, i), h).start()
+        for d in range(2):
+            sib(2 * i - d, step_slot(d, i)).start()
 
     def block_slot(n):
         off = jnp.where(n % 2 == 1, (n + 1) // 2, NZ - n // 2)
@@ -169,14 +174,13 @@
 
     def blocks(n, carry):
         slot = block_slot(n)
-        for h in range(2):
-            sib_in(n, slot, h).wait_recv()
+        sib_in(n, slot).wait_recv()
         for cs in range(2):
             s = cs * NZ + slot
             a = abuf[cs, slot].astype(F32)
             ssq[...] += a[:, :128] * a[:, :128] + a[:, 128:] * a[:, 128:]
             ag = (a * gain_row(s)).astype(BF16)
-            acc[0:256, :] += lax.dot_general(ubuf[s], ag, (((0,), (1,)), ((), ())), preferred_element_type=F32)
+            acc[c, 0:256, :] += lax.dot_general(ubuf[s], ag, (((0,), (1,)), ((), ())), preferred_element_type=F32)
         return carry
 
     def loop_step(i, carry):
@@ -211,8 +215,44 @@
     lax.fori_loop(10, 15, blocks, 0)
     for d in range(2):
         ring_in(d, d, 8).wait_recv()
-        sib(15, (z + 8) % NZ, d).start()
+    sib(15, (z + 8) % NZ).start()
     blocks(15, 0)
+
+    def gather_done():
+        def ring_done(i, carry):
+            for h in range(2):
+                for d in range(2):
+                    ring(d, h, i).wait_send()
+            return carry
+
+        lax.fori_loop(1, 8, ring_done, 0)
+        for d in range(2):
+            ring(d, d, 8).wait_send()
+
+        def sib_done(n, carry):
+            sib(n, block_slot(n)).wait_send()
+            return carry
+
+        lax.fori_loop(0, 16, sib_done, 0)
+
+        @pl.when(mine)
+        def _():
+            def done(k, carry):
+                u_direct(k).wait_send()
+                return carry
+
+            lax.fori_loop(0, 8, done, 0)
+
+        @pl.when(jnp.logical_not(mine))
+        def _():
+            for h in range(2):
+                swap(h).wait_send()
+
+            def done(k, carry):
+                u_mate(k).wait_send()
+                return carry
+
+            lax.fori_loop(0, 8, done, 0)
 
     t_copy.wait_recv()
     t2x = jnp.where(mine, tsrc[0:2, :], tbuf[0:2, :])
@@ -230,11 +270,11 @@
     def is_target(plane):
         return lax.broadcasted_iota(jnp.int32, (256, 512), 0).astype(F32) == tgt - ((plane * NZ + z) * 256).astype(F32)
 
-    logits = acc[0:256, :] * r_row
+    logits = acc[c, 0:256, :] * r_row
     m = jnp.max(logits, axis=0, keepdims=True)
     ex = jnp.exp(logits - m)
-    acc[0:256, :] = ex
-    acc[256:264, :] = jnp.broadcast_to(m, (8, 512))
+    acc[c, 0:256, :] = ex
+    acc[c, 256:264, :] = jnp.broadcast_to(m, (8, 512))
     part_lse = m + jnp.log(jnp.sum(ex, axis=0, keepdims=True))
     part_t = lane_sum(jnp.sum(jnp.where(is_target(c), logits, 0.0), axis=0, keepdims=True) * scale_row)
     zst[z] = jnp.concatenate(as_tile(part_lse) + [part_t] * 4, axis=0)
@@ -254,8 +294,10 @@
         lax.fori_loop(1, NZ, body, 0)
 
     z_all(lambda k: z_copy(k).start())
-    lg_copy = rcopy(acc, accb, lg_sem.at[0], lg_sem.at[1], sibling)
+    lg_copy = rcopy(acc.at[c], acc.at[c], lg_sem.at[0], lg_sem.at[1], sibling)
+    lg_in = rcopy(acc.at[1 - c], acc.at[1 - c], lg_sem.at[0], lg_sem.at[1], sibling)
     lg_copy.start()
+    gather_done()
     weight = scale_row * r_row
     z_all(lambda k: z_in(k).wait_recv())
 
@@ -267,19 +309,16 @@
     le_copy = rcopy(lebuf.at[c], lebuf.at[c], le_sem.at[0], le_sem.at[1], sibling)
     le_in = rcopy(lebuf.at[1 - c], lebuf.at[1 - c], le_sem.at[0], le_sem.at[1], sibling)
     le_copy.start()
-    lg_copy.wait_recv()
+    lg_in.wait_recv()
     le_in.wait_recv()
     l_a, l_b = lebuf[0, 0:4, :], lebuf[1, 0:4, :]
     l_top = jnp.maximum(l_a, l_b)
     lse = l_top + jnp.log(jnp.exp(l_a - l_top) + jnp.exp(l_b - l_top))
     lse_row = jnp.concatenate([lse[k:k + 1, :] for k in range(4)], axis=1)
 
-    def gradient(plane, buf):
-        share = jnp.exp(buf[256:257, :] - lse_row)
-        gbuf[plane] = (weight * (buf[0:256, :] * share - is_target(plane).astype(F32))).astype(BF16)
-
-    gradient(c, acc)
-    gradient(1 - c, accb)
+    def gradient(plane):
+        share = jnp.exp(acc[plane, 256:257, :] - lse_row)
+        gbuf[plane] = (weight * (acc[plane, 0:256, :] * share - is_target(plane).astype(F32))).astype(BF16)
 
     def l_copy(axis, k):
         if axis == 0:
@@ -394,11 +433,14 @@
         for axis in range(2):
             start(axis, o)
 
+    gradient(1 - xh)
     grad_block(2, 2)
     both(start_o, 2)
     for o in (1, 3, 0):
         grad_block(o, 2)
         start_o(0, o)
+    gradient(xh)
+    for o in (1, 3, 0):
         grad_block(2, o)
         start_o(1, o)
     both(start_d, 2)
@@ -429,6 +471,20 @@
             ref[rows, :] = ref[rows, :] + q_o[axis, d]
             send_c2(axis, d).start()
     first_pass(0)
+    loss_end()
+
+    for axis in range(2):
+        for d in range(2):
+            for o in range(4):
+                send_o(axis, d, o).wait_send()
+                send_d(axis, d, o).wait_send()
+                send_c(axis, d, o).wait_send()
+        for k in range(1, 4):
+            l_copy(axis, k).wait_send()
+    for copy in (t_copy, lg_copy, le_copy):
+        copy.wait_send()
+    z_all(lambda k: z_copy(k).wait_send())
+
     s_own = ((y * 2 + xl) * 2 + c) * 2
     gain_own = jnp.concatenate([gain_row(s_own), gain_row(s_own + 1)], axis=1)
     for axis in range(2):
@@ -439,60 +495,11 @@
             fin[rows, :] = (fin[rows, :] + q_c[axis, w].astype(F32) + q_d[axis, 1 - w].astype(F32)) * gain_own
         o_ref[:, 128 * axis:128 * axis + 128] = fin[pl.ds(128 * axis, 128), :].T
 
-    loss_end()
-
     for axis in range(2):
         for d in range(2):
-            for o in range(4):
-                send_o(axis, d, o).wait_send()
-                send_d(axis, d, o).wait_send()
-                send_c(axis, d, o).wait_send()
             send_o2(axis, d).wait_send()
             send_d2(axis, d).wait_send()
             send_c2(axis, d).wait_send()
-    for axis in range(2):
-        for k in range(1, 4):
-            l_copy(axis, k).wait_send()
-    for copy in (t_copy, lg_copy, le_copy):
-        copy.wait_send()
-
-    z_all(lambda k: z_copy(k).wait_send())
-
-    def ring_done(i, carry):
-        for h in range(2):
-            for d in range(2):
-                ring(d, h, i).wait_send()
-        return carry
-
-    lax.fori_loop(1, 8, ring_done, 0)
-    for d in range(2):
-        ring(d, d, 8).wait_send()
-
-    def sib_done(n, carry):
-        for h in range(2):
-            sib(n, block_slot(n), h).wait_send()
-        return carry
-
-    lax.fori_loop(0, 16, sib_done, 0)
-
-    @pl.when(mine)
-    def _():
-        def done(k, carry):
-            u_direct(k).wait_send()
-            return carry
-
-        lax.fori_loop(0, 8, done, 0)
-
-    @pl.when(jnp.logical_not(mine))
-    def _():
-        for h in range(2):
-            swap(h).wait_send()
-
-        def done(k, carry):
-            u_mate(k).wait_send()
-            return carry
-
-        lax.fori_loop(0, 8, done, 0)
 
 
 def per_device(hidden_states, exit_layers, targets, norm_gain, exit_scale, unembedding):
@@ -515,8 +522,7 @@
             dma((5,)),
             pltpu.VMEM((2, 16, 512, 256), BF16),
             pltpu.VMEM((32, 256, 256), BF16),
-            pltpu.VMEM((264, 512), F32),
-            pltpu.VMEM((264, 512), F32),
+            pltpu.VMEM((2, 264, 512), F32),
             pltpu.VMEM((512, 128), F32),
             pltpu.VMEM((2, 256, 512), BF16),
             pltpu.VMEM((8, 128), F32),
@@ -532,7 +538,7 @@
             pltpu.VMEM((2, 2, 64, 512), BF16),
             pltpu.VMEM((2, 2, 64, 512), BF16),
             pltpu.VMEM((2, 2, 64, 512), BF16),
-            dma((2, 2)), dma((2, 2, 8)), dma((2, 2, 8)), dma((16, 2)), dma((16, 2)),
+            dma((2, 2)), dma((2, 2, 8)), dma((2, 2, 8)), dma((16,)), dma((16,)),
             dma((2, 8)), dma((2, 8)), dma, dma((2,)), dma((2,)), dma((16,)), dma((16,)), dma((2,)),
             dma((2, 4)), dma((2, 4)), dma((3, 2, 2, 4)), dma((3, 2, 2, 4)), dma((3, 2, 2)), dma((3, 2, 2)),
         ],

time: 105 us -> 104 us (level)
  no operation moved by 1% of the time
where the time goes in v6:
time: 104 us; the launch traced here: 103 us
  Pallas kernels  100 us (96%)
  between operations  2.33 us (2%)
    pallas_call x1, Pallas kernels, per_device(): pl.pallas_call(kernel, out_shape=(jax.ShapeDtypeStruct((512, 256), F32),...  100 us

profile of v6, /device:TPU:1, one launch (start us, length us, event | category | flops | bytes accessed | tf_op | source)
XLA Modules:
  0.0 103.5 jit_solution(16393731076254089919)
XLA Ops:
  0.6 100.4 %shard_map.77 = (f32[512,256]{1,0:T(8,128)S(1)}, f32[1]{0:T(128)}) custom-call(s32[2,4]{1,0:T(2,128)} %bitcast.7, f32[2]{0:T(128)} %scale_any.1, bf16[4,256,256]{2,1,0:T(8,128)(2,1)} %hid_ref.1, bf16[32,256,256]{2,1,0:T(8,128)(2,1)} %bitcast.5, s32[2,128]{1,0:T(2,128)} %bitcast.8, bf16[64,128]{1,0:T(8,128)(2,1)} %bitcast.6), custom_call_target="tpu_custom_call" | custom-call | tf_op jit(solution)/shard_map/pallas_call | solution.py:510
  101.0 0.8 copy.10

commit v7 on v6

--- a/solution.py
+++ b/solution.py
@@ -175,12 +175,15 @@
     def blocks(n, carry):
         slot = block_slot(n)
         sib_in(n, slot).wait_recv()
+        scaled = []
         for cs in range(2):
-            s = cs * NZ + slot
-            a = abuf[cs, slot].astype(F32)
-            ssq[...] += a[:, :128] * a[:, :128] + a[:, 128:] * a[:, 128:]
-            ag = (a * gain_row(s)).astype(BF16)
-            acc[c, 0:256, :] += lax.dot_general(ubuf[s], ag, (((0,), (1,)), ((), ())), preferred_element_type=F32)
+            a = abuf[cs, slot]
+            wide = a.astype(F32)
+            ssq[...] += wide[:, :128] * wide[:, :128] + wide[:, 128:] * wide[:, 128:]
+            scaled.append(a * gain_row(cs * NZ + slot).astype(BF16))
+        acc[c, 0:256, :] += lax.dot_general(
+            jnp.concatenate([ubuf[slot], ubuf[NZ + slot]], axis=0), jnp.concatenate(scaled, axis=1),
+            (((0,), (1,)), ((), ())), preferred_element_type=F32)
         return carry
 
     def loop_step(i, carry):
@@ -293,7 +296,8 @@
 
         lax.fori_loop(1, NZ, body, 0)
 
-    z_all(lambda k: z_copy(k).start())
+    for k in range(1, NZ):
+        z_copy(k).start()
     lg_copy = rcopy(acc.at[c], acc.at[c], lg_sem.at[0], lg_sem.at[1], sibling)
     lg_in = rcopy(acc.at[1 - c], acc.at[1 - c], lg_sem.at[0], lg_sem.at[1], sibling)
     lg_copy.start()
@@ -443,9 +447,9 @@
     for o in (1, 3, 0):
         grad_block(2, o)
         start_o(1, o)
+    pair_sums(2)
     both(start_d, 2)
     loss_x()
-    pair_sums(2)
     for dy in (1, 3):
         for dx in (1, 3):
             grad_block(dy, dx)

time: 104 us -> 103 us (level)
  no operation moved by 1% of the time
where the time goes in v7:
time: 103 us
  Pallas kernels  100 us (97%)
  between operations  2.33 us (2%)
    pallas_call x1, Pallas kernels, per_device(): pl.pallas_call(kernel, out_shape=(jax.ShapeDtypeStruct((512, 256), F32),...  100 us

profile of v7, /device:TPU:1, one launch (start us, length us, event | category | flops | bytes accessed | tf_op | source)
XLA Modules:
  0.0 103.2 jit_solution(10308073424174987152)
XLA Ops:
  0.6 100.1 %shard_map.77 = (f32[512,256]{1,0:T(8,128)S(1)}, f32[1]{0:T(128)}) custom-call(s32[2,4]{1,0:T(2,128)} %bitcast.7, f32[2]{0:T(128)} %scale_any.1, bf16[4,256,256]{2,1,0:T(8,128)(2,1)} %hid_ref.1, bf16[32,256,256]{2,1,0:T(8,128)(2,1)} %bitcast.5, s32[2,128]{1,0:T(2,128)} %bitcast.8, bf16[64,128]{1,0:T(8,128)(2,1)} %bitcast.6), custom_call_target="tpu_custom_call" | custom-call | tf_op jit(solution)/shard_map/pallas_call | solution.py:514
  100.7 0.8 copy.10

commit v8 on v7

--- a/solution.py
+++ b/solution.py
@@ -453,16 +453,16 @@
     for dy in (1, 3):
         for dx in (1, 3):
             grad_block(dy, dx)
+    pair_sums(1)
     both(start_d, 1)
+    pair_sums(3)
     both(start_d, 3)
-    pair_sums(1)
-    pair_sums(3)
     first_pass(2)
     for k in (1, 3):
         grad_block(0, k)
         grad_block(k, 0)
+    pair_sums(0)
     both(start_d, 0)
-    pair_sums(0)
     loss_y()
     first_pass(1)
     first_pass(3)

time: 103 us -> 103 us (level)
  no operation moved by 1% of the time
where the time goes in v8:
time: 103 us
  Pallas kernels  100 us (97%)
  between operations  2.33 us (2%)
    pallas_call x1, Pallas kernels, per_device(): pl.pallas_call(kernel, out_shape=(jax.ShapeDtypeStruct((512, 256), F32),...  100 us

profile of v8, /device:TPU:1, one launch (start us, length us, event | category | flops | bytes accessed | tf_op | source)
XLA Modules:
  0.0 103.2 jit_solution(10615985506426071587)
XLA Ops:
  0.6 100.1 %shard_map.77 = (f32[512,256]{1,0:T(8,128)S(1)}, f32[1]{0:T(128)}) custom-call(s32[2,4]{1,0:T(2,128)} %bitcast.7, f32[2]{0:T(128)} %scale_any.1, bf16[4,256,256]{2,1,0:T(8,128)(2,1)} %hid_ref.1, bf16[32,256,256]{2,1,0:T(8,128)(2,1)} %bitcast.5, s32[2,128]{1,0:T(2,128)} %bitcast.8, bf16[64,128]{1,0:T(8,128)(2,1)} %bitcast.6), custom_call_target="tpu_custom_call" | custom-call | tf_op jit(solution)/shard_map/pallas_call | solution.py:514
  100.7 0.8 copy.10
